TPU v7x, 256 devices: a whole 4x4x8 slice. The times are simulated.
256 devices in a mesh: section: 4 (over y), expert: 64 (over z, x, core).
Axes of the slice: x: 4, y: 4, z: 8, core: 2. Of those that a mesh axis runs over, the one named last changes fastest.
Arguments:
- front_input: bfloat16 [4, 8192, 3584], P('section', 'expert'), may hold values from -6 to 6
- queries: bfloat16 [4, 8192, 3584], P('section', 'expert'), may hold values from -400 to 400
- keys_values: bfloat16 [4, 8192, 448], P('section', 'expert'), may hold values from -6 to 6
- selected_blocks: int32 [4, 128, 2, 4], P('section', 'expert'), may hold values from 0 to 127, as said below
- front_route: int32 [4, 8192, 1], P('section', 'expert'), may hold values from 0 to 15; in each aligned block of 128 rows (0 to 127, 128 to 255, ..., all dimensions but the last counted through in order) at most 9 rows name the same one
- front_gate: float32 [4, 8192, 1], P('section', 'expert'), may hold values from 0.3 to 1
- back_middle: bfloat16 [4, 8192, 3584], P('section', 'expert'), may hold values from -6 to 6
- back_grad: bfloat16 [4, 8192, 3584], P('section', 'expert'), may hold values from -6 to 6
- back_route: int32 [4, 8192, 1], P('section', 'expert'), may hold values from 0 to 15; in each aligned block of 128 rows (0 to 127, 128 to 255, ..., all dimensions but the last counted through in order) at most 9 rows name the same one
- back_gate: float32 [4, 8192, 1], P('section', 'expert'), may hold values from 0.3 to 1
- norm_gain: float32 [4, 3584], P('section'), may hold values from 0.1 to 1.9
- gate_slice: bfloat16 [4, 64, 3584, 256], P('section', 'expert'), may hold values from -0.09375 to 0.09375
- up_slice: bfloat16 [4, 64, 3584, 256], P('section', 'expert'), may hold values from -0.09375 to 0.09375
- down_slice: bfloat16 [4, 64, 256, 3584], P('section', 'expert'), may hold values from -0.1875 to 0.1875
Outputs:
- front_output: bfloat16 [4, 8192, 3584], P('section', 'expert')
- back_output: bfloat16 [4, 8192, 3584], P('section', 'expert')
Inputs may be any that keep to these rules, and one draw needn't show every extreme that they name: `selected_blocks`: each list holds 4 different block numbers, among them the query block's own; the others are at most the larger of the query block's number and 3. `front_route`: in the tokens of one device at one section, no expert is named more than 9 times. `back_route`: in the tokens of one device at one section, no expert is named more than 9 times.
All inputs are finite; a program needn't handle non-finite values.
Results may differ from a plain program's by a relative error of at most 0.0057.
Values may be sent and summed in bfloat16 or wider, within the bound.
A program may use at most 192 MiB of HBM per device.

v0:
```python
import jax
import jax.numpy as jnp
from jax import lax
from jax.sharding import PartitionSpec as P

GROUP = 4
HEADS = 32
HEAD_DIM = 112
KV_HEADS = 2
BLK = 64


epsilon = 1e-06
negative_large = -1e30


def passed_along(array, axis, by):
    length = lax.axis_size(axis)
    return lax.ppermute(array, axis, [(i, (i + by) % length) for i in range(length)])


def rms_scale(rows):
    return lax.rsqrt(jnp.mean(rows * rows, axis=-1, keepdims=True) + epsilon)


def attend_local(query_rows, kv_rows, chosen_blocks):
    gathered = lax.all_gather(kv_rows, "expert", axis=0, tiled=True)
    block_count = gathered.shape[0] // BLK
    blocks_view = gathered.reshape(block_count, BLK, 2, KV_HEADS, HEAD_DIM)
    groups = HEADS // KV_HEADS
    query_blocks = query_rows.reshape(-1, BLK, KV_HEADS, groups, HEAD_DIM)
    local_blocks = query_blocks.shape[0]
    first_block = lax.axis_index("expert") * local_blocks
    head_index = jnp.arange(KV_HEADS, dtype=jnp.int32)[:, None]
    offsets = jnp.arange(BLK, dtype=jnp.int32)

    def one_block(query_block, chosen, block_index):
        key_sel = blocks_view[chosen, :, 0, head_index].reshape(KV_HEADS, -1, HEAD_DIM)
        value_sel = blocks_view[chosen, :, 1, head_index].reshape(KV_HEADS, -1, HEAD_DIM)
        scores = jnp.einsum(
            "qhgd,hkd->hgqk", query_block, key_sel, preferred_element_type=jnp.float32
        ) * HEAD_DIM ** (-0.5)
        key_pos = (chosen[:, :, None] * BLK + offsets[None, None, :]).reshape(KV_HEADS, -1)
        query_pos = block_index * BLK + offsets
        allowed = key_pos[:, None, None, :] <= query_pos[None, None, :, None]
        scores = jnp.where(allowed, scores, negative_large)
        row_max = jnp.max(scores, axis=-1, keepdims=True)
        exp_scores = jnp.exp(scores - row_max)
        row_total = jnp.sum(exp_scores, axis=-1, keepdims=True)
        attention_weights = (exp_scores / row_total).astype(jnp.bfloat16)
        mixed_out = jnp.einsum(
            "hgqk,hkd->qhgd", attention_weights, value_sel, preferred_element_type=jnp.float32
        )
        return mixed_out.reshape(BLK, HEADS * HEAD_DIM)

    attended = jax.vmap(one_block)(
        query_blocks, chosen_blocks, first_block + jnp.arange(local_blocks, dtype=jnp.int32)
    )
    return attended.reshape(query_rows.shape[0], HEADS * HEAD_DIM)


def place_rows(route, experts, capacity):
    flat_route = route.reshape(-1)
    onehot = (flat_route[:, None] == jnp.arange(experts, dtype=jnp.int32)[None, :]).astype(
        jnp.int32
    )
    before = jnp.cumsum(onehot, axis=0) - onehot
    return flat_route * capacity + jnp.sum(before * onehot, axis=1)


def pack_rows(rows, destination, experts, capacity):
    feature_width = rows.shape[1]
    buffer = jnp.zeros((experts * capacity, feature_width), rows.dtype).at[destination].set(rows)
    return jnp.repeat(buffer.reshape(experts, capacity, feature_width), GROUP, axis=0)


def unpack_rows(returned, destination, experts, capacity):
    feature_width = returned.shape[2]
    grid = returned.reshape(experts, GROUP, capacity, feature_width)
    picked = grid[destination // capacity, :, destination % capacity]
    return jnp.sum(picked.astype(jnp.float32), axis=1)


def slice_forward(rows, w_gate, w_up, w_down):
    gate_val = jnp.dot(rows, w_gate, preferred_element_type=jnp.float32)
    up_val = jnp.dot(rows, w_up, preferred_element_type=jnp.float32)
    hidden = (jax.nn.silu(gate_val) * up_val).astype(jnp.bfloat16)
    return jnp.dot(hidden, w_down, preferred_element_type=jnp.float32).astype(jnp.bfloat16)


def slice_backward(rows, grads, w_gate, w_up, w_down):
    contract_last = (((1,), (1,)), ((), ()))
    gate_val = jnp.dot(rows, w_gate, preferred_element_type=jnp.float32)
    up_val = jnp.dot(rows, w_up, preferred_element_type=jnp.float32)
    sigmoid_val = jax.nn.sigmoid(gate_val)
    act_val = gate_val * sigmoid_val
    slope_val = sigmoid_val * (1.0 + gate_val * (1.0 - sigmoid_val))
    down_back = lax.dot_general(grads, w_down, contract_last, preferred_element_type=jnp.float32)
    gate_grad = (down_back * up_val * slope_val).astype(jnp.bfloat16)
    up_grad = (down_back * act_val).astype(jnp.bfloat16)
    both_grad = jnp.concatenate([gate_grad, up_grad], axis=1)
    both_weight = jnp.concatenate([w_gate, w_up], axis=1)
    total_val = lax.dot_general(
        both_grad, both_weight, contract_last, preferred_element_type=jnp.float32
    )
    return total_val.astype(jnp.bfloat16)


def shards(
    front_input,
    queries,
    keys_values,
    selected_blocks,
    front_route,
    front_gate,
    back_middle,
    back_grad,
    back_route,
    back_gate,
    norm_gain,
    gate_slice,
    up_slice,
    down_slice,
):
    feature_width = front_input.shape[2]
    tokens_here = front_input.shape[1]
    routes_per = front_route.shape[2]
    experts = lax.axis_size("expert") // GROUP
    average = tokens_here * routes_per // experts
    capacity = average + max(1, average // 8)
    w_gate = gate_slice[0, 0]
    w_up = up_slice[0, 0]
    w_down = down_slice[0, 0]
    gain_row = norm_gain[0]
    attention_out = attend_local(queries[0], keys_values[0], selected_blocks[0])
    middle = (front_input[0].astype(jnp.float32) + attention_out).astype(jnp.bfloat16)
    middle = lax.optimization_barrier(middle).astype(jnp.float32)
    normed = (middle * rms_scale(middle) * gain_row).astype(jnp.bfloat16)
    front_rows = jnp.repeat(normed, routes_per, axis=0)
    back_mid = back_middle[0].astype(jnp.float32)
    back_scale = rms_scale(back_mid)
    back_normed = (back_mid * back_scale * gain_row).astype(jnp.bfloat16)
    grad_rows = jnp.repeat(back_grad[0].astype(jnp.float32), routes_per, axis=0)
    scaled = (back_gate[0] * grad_rows).astype(jnp.bfloat16)
    back_rows = jnp.repeat(back_normed, routes_per, axis=0)
    front_dest = place_rows(front_route[0], experts, capacity)
    back_dest = place_rows(back_route[0], experts, capacity)
    front_send = pack_rows(front_rows, front_dest, experts, capacity)
    back_send_rows = pack_rows(back_rows, back_dest, experts, capacity)
    back_send_grads = pack_rows(scaled, back_dest, experts, capacity)
    received = lax.all_to_all(front_send, "expert", split_axis=0, concat_axis=0, tiled=True)
    partial_value = slice_forward(received.reshape(-1, feature_width), w_gate, w_up, w_down)
    front_return = lax.all_to_all(
        partial_value.reshape(received.shape), "expert", split_axis=0, concat_axis=0, tiled=True
    )
    received = (
        lax.all_to_all(back_send_rows, "expert", split_axis=0, concat_axis=0, tiled=True),
        lax.all_to_all(back_send_grads, "expert", split_axis=0, concat_axis=0, tiled=True),
    )
    received_rows = received[0]
    partial_value = slice_backward(
        received_rows.reshape(-1, feature_width),
        received[1].reshape(-1, feature_width),
        w_gate,
        w_up,
        w_down,
    )
    back_return = lax.all_to_all(
        partial_value.reshape(received_rows.shape),
        "expert",
        split_axis=0,
        concat_axis=0,
        tiled=True,
    )
    expert_out = unpack_rows(front_return, front_dest, experts, capacity)
    expert_grad = unpack_rows(back_return, back_dest, experts, capacity)
    weighted = expert_out * front_gate[0]
    contrib = jnp.sum(weighted.reshape(tokens_here, routes_per, feature_width), axis=1)
    front_result = (middle + contrib).astype(jnp.bfloat16)
    normed_grad = jnp.sum(expert_grad.reshape(tokens_here, routes_per, feature_width), axis=1)
    amount = gain_row * normed_grad
    cube = back_scale * back_scale * back_scale
    back_result = (
        back_grad[0].astype(jnp.float32)
        + back_scale * amount
        - back_mid * cube * jnp.mean(back_mid * amount, axis=-1, keepdims=True)
    )
    back_result = back_result.astype(jnp.bfloat16)
    front_output = passed_along(front_result, "section", 1)
    back_output = passed_along(back_result, "section", -1)
    return (front_output[None], back_output[None])


def solution(mesh):
    placed = (
        P("section", "expert", None),
        P("section", "expert", None),
        P("section", "expert", None),
        P("section", "expert", None, None),
        P("section", "expert", None),
        P("section", "expert", None),
        P("section", "expert", None),
        P("section", "expert", None),
        P("section", "expert", None),
        P("section", "expert", None),
        P("section", None),
        P("section", "expert", None, None),
        P("section", "expert", None, None),
        P("section", "expert", None, None),
    )
    return jax.shard_map(
        shards,
        mesh=mesh,
        in_specs=placed,
        out_specs=(P("section", "expert", None), P("section", "expert", None)),
        check_vma=False,
    )
```

profile of v0, /device:TPU:34, one launch (start us, length us, event | category | flops | bytes accessed | tf_op | source)
XLA Modules:
  0.0 966.7 jit_solution(12022570513743927064)
XLA Ops:
  18.8 5.4 broadcast_in_dim.33
  24.2 11.9 %all-to-all-start.3 = ((bf16[64,9,3584]{2,1,0:T(8,128)(2,1)}), bf16[64,9,3584]{2,1,0:T(8,128)(2,1)}, u32[]{:S(2)}, u32[]{:S(2)}) async-start(bf16[64,9,3584]{2,1,0:T(8,128)(2,1)} %bitcast.128), calls=%async_computation.3 | async-start | bytes 14680064 | tf_op jit(solution)/shard_map/all_to_all | solution.py:157
  41.6 177.0 %all-to-all-done.3 = bf16[64,9,3584]{2,1,0:T(8,128)(2,1)} async-done(((bf16[64,9,3584]{2,1,0:T(8,128)(2,1)}), bf16[64,9,3584]{2,1,0:T(8,128)(2,1)}, u32[]{:S(2)}, u32[]{:S(2)}) %all-to-all-start.3) | async-done | bytes 4128800 | tf_op jit(solution)/shard_map/all_to_all | solution.py:157
  218.6 5.3 broadcast_in_dim.32
  223.9 6.6 all-to-all-start.2
  234.2 20.9 %reshape.452 = bf16[128,64,2,2,112]{1,0,4,3,2:T(8,128)(2,1)} reshape(bf16[1,8192,448]{1,2,0:T(8,128)(2,1)} %all-gather.3.cloned.1.call-done) | data formatting | bytes 14680064 | tf_op jit(solution)/shard_map/reshape | solution.py:29
  255.1 17.3 %copy.25 = bf16[128,64,2,2,112]{4,1,3,2,0:T(8,128)(2,1)} copy(bf16[128,64,2,2,112]{1,0,4,3,2:T(8,128)(2,1)} %reshape.452) | data formatting | bytes 14680064 | tf_op jit(solution)/shard_map/reshape | solution.py:29
  272.4 4.0 gather_fusion
  276.4 4.0 gather_fusion.1
  299.5 94.4 %all-to-all-done.2 = bf16[64,9,3584]{2,1,0:T(8,128)(2,1)} async-done(((bf16[64,9,3584]{2,1,0:T(8,128)(2,1)}), bf16[64,9,3584]{2,1,0:T(8,128)(2,1)}, u32[]{:S(2)}, u32[]{:S(2)}) %all-to-all-start.2) | async-done | bytes 4128800 | tf_op jit(solution)/shard_map/all_to_all | solution.py:158
  393.9 5.4 broadcast_in_dim.30
  399.3 6.8 all-to-all-start
  406.1 7.9 reshape.392
  414.1 7.9 reshape.389
  422.0 4.1 fusion.79
  430.4 4.3 convolution_convert_fusion
  434.7 7.6 reshape.393
  442.3 127.1 %all-to-all-done = bf16[64,9,3584]{2,1,0:T(8,128)(2,1)} async-done(((bf16[64,9,3584]{2,1,0:T(8,128)(2,1)}), bf16[64,9,3584]{2,1,0:T(8,128)(2,1)}, u32[]{:S(2)}, u32[]{:S(2)}) %all-to-all-start) | async-done | bytes 4128800 | tf_op jit(solution)/shard_map/all_to_all | solution.py:151
  569.5 6.3 all-to-all-start.4
  575.8 8.0 reshape.384
  587.8 9.2 convolution_convert_fusion.1
  597.0 7.7 reshape.385
  604.6 134.6 %all-to-all-done.4 = bf16[64,9,3584]{2,1,0:T(8,128)(2,1)} async-done(((bf16[64,9,3584]{2,1,0:T(8,128)(2,1)}), bf16[64,9,3584]{2,1,0:T(8,128)(2,1)}, u32[]{:S(2)}, u32[]{:S(2)}) %all-to-all-start.4) | async-done | bytes 4128800 | tf_op jit(solution)/shard_map/all_to_all | solution.py:168
  739.2 6.5 all-to-all-start.1
  745.7 8.8 copy.34
  754.5 7.6 gather_fusion.3
  762.2 7.3 convert_reduce_fusion
  775.7 133.3 %all-to-all-done.1 = bf16[64,9,3584]{2,1,0:T(8,128)(2,1)} async-done(((bf16[64,9,3584]{2,1,0:T(8,128)(2,1)}), bf16[64,9,3584]{2,1,0:T(8,128)(2,1)}, u32[]{:S(2)}, u32[]{:S(2)}) %all-to-all-start.1) | async-done | bytes 4128800 | tf_op jit(solution)/shard_map/all_to_all | solution.py:153
  909.0 8.7 copy.32
  917.7 7.6 gather_fusion.2
  925.3 7.3 convert_reduce_fusion.1
  934.6 21.9 %collective-permute-done = bf16[128,3584]{1,0:T(8,128)(2,1)S(1)} collective-permute-done((bf16[128,3584]{1,0:T(8,128)(2,1)S(1)}, bf16[128,3584]{1,0:T(8,128)(2,1)S(1)}, u32[]{:S(2)}, u32[]{:S(2)}) %collective-permute-start) | collective-permute-done | bytes 917536 | tf_op jit(solution)/shard_map/ppermute | solution.py:19
  (79 shorter events, 59.4 us)
Async XLA Ops:
  7.2 418.9 %copy-start = (bf16[1,1,256,3584]{3,2,1,0:T(8,128)(2,1)S(1)}, bf16[1,1,256,3584]{3,2,1,0:T(8,128)(2,1)}, u32[]{:S(2)}) copy-start(bf16[1,1,256,3584]{3,2,1,0:T(8,128)(2,1)} %param.27) | copy-start | bytes 5505028
  7.2 227.0 %all-gather.3.cloned.1.call-start = ((), (), s32[]{:S(2)}) async-start(), calls=%async_computation.5 | async-start | bytes 7454720 | tf_op jit(solution)/shard_map/all_gather | solution.py:27
  24.2 11.9 %copy-start.4 = (bf16[1,128,3584]{2,1,0:T(8,128)(2,1)S(1)}, bf16[1,128,3584]{2,1,0:T(8,128)(2,1)}, u32[]{:S(2)}) copy-start(bf16[1,128,3584]{2,1,0:T(8,128)(2,1)} %param.21) | copy-start | bytes 2752516
  24.2 11.9 %copy-start.9 = (f32[1,128,1]{1,2,0:T(1,128)S(1)}, f32[1,128,1]{1,2,0:T(1,128)}, u32[]{:S(2)}) copy-start(f32[1,128,1]{1,2,0:T(1,128)} %param.23) | copy-start | bytes 1540
  24.2 194.4 %all-to-all-start.3 = ((bf16[64,9,3584]{2,1,0:T(8,128)(2,1)}), bf16[64,9,3584]{2,1,0:T(8,128)(2,1)}, u32[]{:S(2)}, u32[]{:S(2)}) async-start(bf16[64,9,3584]{2,1,0:T(8,128)(2,1)} %bitcast.128), calls=%async_computation.3 | async-start | bytes 14680064 | tf_op jit(solution)/shard_map/all_to_all | solution.py:157
  223.9 6.6 copy-start.7
  223.9 6.8 copy-start.6
  223.9 9.5 copy-start.8
  223.9 170.0 %all-to-all-start.2 = ((bf16[64,9,3584]{2,1,0:T(8,128)(2,1)}), bf16[64,9,3584]{2,1,0:T(8,128)(2,1)}, u32[]{:S(2)}, u32[]{:S(2)}) async-start(bf16[64,9,3584]{2,1,0:T(8,128)(2,1)} %bitcast.126), calls=%async_computation.2 | async-start | bytes 14680064 | tf_op jit(solution)/shard_map/all_to_all | solution.py:158
  399.3 170.2 %all-to-all-start = ((bf16[64,9,3584]{2,1,0:T(8,128)(2,1)}), bf16[64,9,3584]{2,1,0:T(8,128)(2,1)}, u32[]{:S(2)}, u32[]{:S(2)}) async-start(bf16[64,9,3584]{2,1,0:T(8,128)(2,1)} %bitcast.127), calls=%async_computation | async-start | bytes 14680064 | tf_op jit(solution)/shard_map/all_to_all | solution.py:151
  422.0 4.1 copy-start.3
  426.1 2.2 copy-start.2
  426.1 2.7 copy-start.12
  428.9 1.5 copy-start.11
  569.5 169.7 %all-to-all-start.4 = ((bf16[64,9,3584]{2,1,0:T(8,128)(2,1)}), bf16[64,9,3584]{2,1,0:T(8,128)(2,1)}, u32[]{:S(2)}, u32[]{:S(2)}) async-start(bf16[64,9,3584]{2,1,0:T(8,128)(2,1)} %reshape.393), calls=%async_computation.4 | async-start | bytes 14680064 | tf_op jit(solution)/shard_map/all_to_all | solution.py:168
  739.2 169.8 %all-to-all-start.1 = ((bf16[64,9,3584]{2,1,0:T(8,128)(2,1)}), bf16[64,9,3584]{2,1,0:T(8,128)(2,1)}, u32[]{:S(2)}, u32[]{:S(2)}) async-start(bf16[64,9,3584]{2,1,0:T(8,128)(2,1)} %reshape.385), calls=%async_computation.1 | async-start | bytes 14680064 | tf_op jit(solution)/shard_map/all_to_all | solution.py:153
  762.1 7.3 copy-start.1
  769.5 1.2 copy-start.5
  772.4 162.2 %collective-permute-start.1 = (bf16[128,3584]{1,0:T(8,128)(2,1)}, bf16[128,3584]{1,0:T(8,128)(2,1)}, u32[]{:S(2)}, u32[]{:S(2)}) collective-permute-start(bf16[128,3584]{1,0:T(8,128)(2,1)} %fusion.11), channel_id=1, source_target_pairs={{0,192},{64,0},{128,64},{192,128},{1,193},{65,1},{129,65},{193,129... | collective-permute-start | bytes 2752520 | tf_op jit(solution)/shard_map/ppermute | solution.py:19
  925.3 7.3 copy-start.10
  932.9 23.7 %collective-permute-start = (bf16[128,3584]{1,0:T(8,128)(2,1)S(1)}, bf16[128,3584]{1,0:T(8,128)(2,1)S(1)}, u32[]{:S(2)}, u32[]{:S(2)}) collective-permute-start(bf16[128,3584]{1,0:T(8,128)(2,1)S(1)} %fusion.15), channel_id=1, source_target_pairs={{0,64},{64,128},{128,192},{192,0},{1,65},{65,129},{129,193},{193,1... | collective-permute-start | bytes 2752520 | tf_op jit(solution)/shard_map/ppermute | solution.py:19
Sparse Core Ops, SparseCore 0:
  10.7 155.5 all-gather.2
where the time goes:
time: 975 us; the launch traced here: 967 us
  waiting for transfers between devices  689 us (71%)
  local copies, waits for them, and re-layouts  156 us (16%)
  starting transfers between devices  43.2 us (4%)
  other arithmetic  36 us (4%)
  matrix products  27.6 us (3%)
  between operations  14.6 us (1%)
    all_to_all x1, waiting for transfers between devices, shards(): lax.all_to_all(back_send_rows, 'expert', split_axis=0, concat_axis=0, til...  177 us
    all_to_all x1, waiting for transfers between devices, shards(): lax.all_to_all(partial_value.reshape(received_rows.shape), 'expert', spli...  135 us
    all_to_all x1, waiting for transfers between devices, shards(): lax.all_to_all(partial_value.reshape(received.shape), 'expert', split_axi...  133 us
    all_to_all x1, waiting for transfers between devices, shards(): lax.all_to_all(front_send, 'expert', split_axis=0, concat_axis=0, tiled=T...  127 us
    all_to_all x1, waiting for transfers between devices, shards(): lax.all_to_all(back_send_grads, 'expert', split_axis=0, concat_axis=0, ti...  94.4 us
    reshape x2, local copies, waits for them, and re-layouts, attend_local(): blocks_view = gathered.reshape(block_count, BLK, 2, KV_HEADS, HEAD_DIM)  38.2 us
    ppermute x2, waiting for transfers between devices, passed_along(): lax.ppermute(array, axis, [(i, (i + by) % length) for i in range(length)])  21.9 us
  transfers between devices with their start and end apart: 8, of which 6 were waited for; matrix products, arithmetic and copies ran while one was open for 22% of the time, Pallas kernels for 0%

commit v1 on v0

v1 whole, which is shorter than its diff:
```python
import functools

import jax
import jax.numpy as jnp
from jax import lax
from jax.experimental import pallas as pl
from jax.experimental.pallas import tpu as pltpu
from jax.sharding import PartitionSpec as P

HEADS = 32
HEAD_DIM = 112
KV_HEADS = 2
GROUPS = HEADS // KV_HEADS
BLK = 64
SEL = 4
QUARTERS = 4
NX = 4
EPS = 1e-06
NEG = -1e30
MESH = pl.DeviceIdType.MESH
BF = jnp.bfloat16
F32 = jnp.float32


def iota(shape, dim):
    return lax.broadcasted_iota(jnp.int32, shape, dim)


def slot_row(route, experts):
    tokens = route.shape[1]
    onehot = jnp.where(iota((experts, tokens), 0) == route, 1.0, 0.0)
    earlier = jnp.where(iota((tokens, tokens), 0) < iota((tokens, tokens), 1), 1.0, 0.0)
    before = jnp.dot(onehot.astype(BF), earlier.astype(BF), preferred_element_type=F32)
    return jnp.sum(before * onehot, axis=0, keepdims=True).astype(jnp.int32)


def main_onehot(route, slot, experts):
    place = jnp.where(slot < 8, route * 8 + slot, -1)
    return jnp.where(iota((experts * 8, route.shape[1]), 0) == place, 1.0, 0.0)


def tail_onehot(route, slot, experts, quarter):
    place = jnp.where(slot >= 8, route * 4 + quarter, -1)
    return jnp.where(iota((experts * 4, route.shape[1]), 0) == place, 1.0, 0.0)


def pack(route, experts, rows_of, send_ref):
    slot = slot_row(route, experts)
    main = main_onehot(route, slot, experts).astype(BF)
    planes = experts // 2
    tail = None
    for q in range(QUARTERS):
        rows = rows_of(q)
        width = rows.shape[1]
        sorted_rows = jnp.dot(main, rows, preferred_element_type=F32).reshape(planes, 2, 8, width)
        send_ref[:, q] = sorted_rows[:, 0].astype(BF)
        send_ref[:, 5 + q] = sorted_rows[:, 1].astype(BF)
        last = jnp.dot(
            tail_onehot(route, slot, experts, q).astype(BF), rows, preferred_element_type=F32
        )
        tail = last if tail is None else tail + last
    send_ref[:, 4] = tail.reshape(planes, 8, width).astype(BF)


def unpack(route, experts, back_ref):
    slot = slot_row(route, experts)
    main = main_onehot(route, slot, experts).T.astype(BF)
    planes = experts // 2
    width = back_ref.shape[3]

    def rows_of(q):
        first = back_ref[:, q].astype(F32)
        second = back_ref[:, 5 + q].astype(F32)
        both = jnp.stack([first, second], axis=1).reshape(experts * 8, width).astype(BF)
        last = back_ref[:, 4].astype(F32).reshape(planes * 8, width).astype(BF)
        tail = tail_onehot(route, slot, experts, q).T.astype(BF)
        return jnp.dot(main, both, preferred_element_type=F32) + jnp.dot(
            tail, last, preferred_element_type=F32
        )

    return rows_of


def quarter(q, width):
    return slice(q * width, (q + 1) * width)


def back_pack_kernel(mid_ref, grad_ref, gain_ref, gate_ref, route_ref, rows_ref, grads_ref):
    experts = rows_ref.shape[0] * 2
    width = rows_ref.shape[3]
    mid = mid_ref[...].astype(F32)
    scale = lax.rsqrt(jnp.mean(mid * mid, axis=-1, keepdims=True) + EPS)
    tokens = mid.shape[0]
    gate = jnp.broadcast_to(gate_ref[...], (tokens, tokens)).T[:, 0:1]
    route = route_ref[...]

    def normed(q):
        part = mid_ref[:, quarter(q, width)].astype(F32)
        return (part * scale * gain_ref[:, quarter(q, width)]).astype(BF)

    def scaled(q):
        return (gate * grad_ref[:, quarter(q, width)].astype(F32)).astype(BF)

    pack(route, experts, normed, rows_ref)
    pack(route, experts, scaled, grads_ref)


def attention_kernel(
    sel_ref, query_ref, kv_ref, input_ref, gain_ref, route_ref,
    middle_ref, send_ref, kbuf, vbuf, total, sem,
):
    experts = send_ref.shape[0] * 2
    width = send_ref.shape[3]
    tokens = query_ref.shape[0]
    blocks = tokens // BLK
    first = sel_ref[blocks * KV_HEADS * SEL]
    copies = []
    for b in range(blocks):
        for h in range(KV_HEADS):
            for k in range(SEL):
                index = (b * KV_HEADS + h) * SEL + k
                chosen = sel_ref[index]
                owner = chosen // blocks
                rows = pl.ds(pl.multiple_of((chosen % blocks) * BLK, BLK), BLK)
                for w, buf in enumerate((kbuf, vbuf)):
                    copy = pltpu.make_async_copy(
                        kv_ref.at[owner, 2 * w + h, rows],
                        buf.at[b * KV_HEADS + h, pl.ds(k * BLK, BLK)],
                        sem.at[w, index],
                    )
                    copy.start()
                    copies.append(copy)
    total[...] = jnp.zeros_like(total)
    for copy in copies:
        copy.wait()
    keys = SEL * BLK
    for b in range(blocks):
        token_rows = slice(b * BLK, (b + 1) * BLK)
        query_pos = (first + b) * BLK + iota((2 * BLK, keys), 0) % BLK
        for h in range(KV_HEADS):
            pair = b * KV_HEADS + h
            lane = iota((2 * BLK, keys), 1)
            key_pos = lane % BLK
            for k in range(SEL):
                key_pos = key_pos + jnp.where(
                    lane // BLK == k, sel_ref[pair * SEL + k] * BLK, 0
                )
            allowed = key_pos <= query_pos
            key_rows = kbuf[pair]
            value_rows = vbuf[pair]
            for g in range(GROUPS // 2):
                offset = (HEAD_DIM * g) % 128
                window = 128 if offset + HEAD_DIM <= 128 else 256
                at = iota((128, window), 0)
                shift = jnp.where(
                    (iota((128, window), 1) == at + offset) & (at < HEAD_DIM), 1.0, 0.0
                ).astype(BF)
                key_moved = jnp.dot(key_rows, shift, preferred_element_type=F32).astype(BF)
                value_moved = jnp.dot(value_rows, shift, preferred_element_type=F32).astype(BF)
                starts = []
                for half in range(2):
                    head = h * GROUPS + g + half * (GROUPS // 2)
                    starts.append(HEAD_DIM * head // 128 * 128)
                query = jnp.concatenate(
                    [query_ref[token_rows, s : s + window] for s in starts], axis=0
                )
                scores = lax.dot_general(
                    query, key_moved, (((1,), (1,)), ((), ())), preferred_element_type=F32
                ) * HEAD_DIM ** (-0.5)
                scores = jnp.where(allowed, scores, NEG)
                exp_scores = jnp.exp(scores - jnp.max(scores, axis=-1, keepdims=True))
                weights = exp_scores / jnp.sum(exp_scores, axis=-1, keepdims=True)
                mixed = jnp.dot(weights.astype(BF), value_moved, preferred_element_type=F32)
                for half, s in enumerate(starts):
                    total[token_rows, s : s + window] += mixed[half * BLK : (half + 1) * BLK]
    squares = jnp.zeros((tokens, 1), F32)
    for q in range(QUARTERS):
        cols = quarter(q, width)
        middle = (input_ref[:, cols].astype(F32) + total[:, cols]).astype(BF)
        middle_ref[:, cols] = middle
        middle = middle.astype(F32)
        squares += jnp.sum(middle * middle, axis=-1, keepdims=True)
    scale = lax.rsqrt(squares / query_ref.shape[1] + EPS)

    def normed(q):
        cols = quarter(q, width)
        return (middle_ref[:, cols].astype(F32) * scale * gain_ref[:, cols]).astype(BF)

    pack(route_ref[...], experts, normed, send_ref)


def tail_select(count, h, q):
    row, col = iota((count, count * 8), 0), iota((count, count * 8), 1)
    return jnp.where(col == row * 8 + h * 4 + q, 1.0, 0.0).astype(BF)


def rows_for_expert(recv_ref, h, q):
    count, width = recv_ref.shape[0], recv_ref.shape[3]
    main = recv_ref[:, q + h].astype(F32).reshape(count * 8, width).astype(BF)
    last = recv_ref[:, 4 - 4 * h].astype(F32).reshape(count * 8, width).astype(BF)
    tail = jnp.dot(tail_select(count, h, q), last, preferred_element_type=F32).astype(BF)
    return jnp.concatenate([main, tail], axis=0)


def store_for_source(out_ref, h, q, value, tail_total):
    count, width = out_ref.shape[0], out_ref.shape[3]
    out_ref[:, q + h] = value[: count * 8].reshape(count, 8, width).astype(BF)
    spread = lax.dot_general(
        tail_select(count, h, q), value[count * 8 :].astype(BF),
        (((0,), (0,)), ((), ())), preferred_element_type=F32,
    )
    return spread if tail_total is None else tail_total + spread


def forward_kernel(h_ref, recv_ref, g0, u0, d0, g1, u1, d1, out_ref):
    h = h_ref[0]
    width = recv_ref.shape[3]
    sides = ((g0, u0, d0), (g1, u1, d1))
    gates, ups = [None, None], [None, None]
    for q in range(QUARTERS):
        rows = rows_for_expert(recv_ref, h, q)
        part = quarter(q, width)
        for i, (g, u, _) in enumerate(sides):
            gate = jnp.dot(rows, g[part], preferred_element_type=F32)
            up = jnp.dot(rows, u[part], preferred_element_type=F32)
            gates[i] = gate if gates[i] is None else gates[i] + gate
            ups[i] = up if ups[i] is None else ups[i] + up
    hidden = [(v / (1.0 + jnp.exp(-v)) * u).astype(BF) for v, u in zip(gates, ups)]
    tail = None
    for q in range(QUARTERS):
        part = quarter(q, width)
        value = jnp.dot(hidden[0], d0[:, part], preferred_element_type=F32) + jnp.dot(
            hidden[1], d1[:, part], preferred_element_type=F32
        )
        tail = store_for_source(out_ref, h, q, value, tail)
    out_ref[:, 4 - 4 * h] = tail.reshape(out_ref.shape[0], 8, width).astype(BF)


def backward_kernel(h_ref, recv_ref, recv_grad_ref, g0, u0, d0, g1, u1, d1, out_ref):
    h = h_ref[0]
    width = recv_ref.shape[3]
    last = (((1,), (1,)), ((), ()))
    sides = ((g0, u0, d0), (g1, u1, d1))
    gates, ups, downs = [None, None], [None, None], [None, None]
    for q in range(QUARTERS):
        rows = rows_for_expert(recv_ref, h, q)
        grads = rows_for_expert(recv_grad_ref, h, q)
        part = quarter(q, width)
        for i, (g, u, d) in enumerate(sides):
            gate = jnp.dot(rows, g[part], preferred_element_type=F32)
            up = jnp.dot(rows, u[part], preferred_element_type=F32)
            down = lax.dot_general(grads, d[:, part], last, preferred_element_type=F32)
            gates[i] = gate if gates[i] is None else gates[i] + gate
            ups[i] = up if ups[i] is None else ups[i] + up
            downs[i] = down if downs[i] is None else downs[i] + down
    gate_grads, up_grads = [], []
    for gate, up, down in zip(gates, ups, downs):
        sigmoid = 1.0 / (1.0 + jnp.exp(-gate))
        gate_grads.append((down * up * (sigmoid * (1.0 + gate * (1.0 - sigmoid)))).astype(BF))
        up_grads.append((down * (gate * sigmoid)).astype(BF))
    tail = None
    for q in range(QUARTERS):
        part = quarter(q, width)
        value = None
        for i, (g, u, _) in enumerate(sides):
            more = lax.dot_general(
                gate_grads[i], g[part], last, preferred_element_type=F32
            ) + lax.dot_general(up_grads[i], u[part], last, preferred_element_type=F32)
            value = more if value is None else value + more
        tail = store_for_source(out_ref, h, q, value, tail)
    out_ref[:, 4 - 4 * h] = tail.reshape(out_ref.shape[0], 8, width).astype(BF)


def front_last_kernel(middle_ref, back_ref, meta_ref, out_ref):
    experts = back_ref.shape[0] * 2
    width = back_ref.shape[3]
    tokens = middle_ref.shape[0]
    gate = jnp.broadcast_to(meta_ref[0:1], (tokens, tokens)).T[:, 0:1]
    rows_of = unpack(meta_ref[1:2].astype(jnp.int32), experts, back_ref)
    for q in range(QUARTERS):
        cols = quarter(q, width)
        out_ref[:, cols] = (middle_ref[:, cols].astype(F32) + gate * rows_of(q)).astype(BF)


def back_last_kernel(mid_ref, grad_ref, gain_ref, back_ref, meta_ref, out_ref, amount):
    experts = back_ref.shape[0] * 2
    width = back_ref.shape[3]
    features = mid_ref.shape[1]
    rows_of = unpack(meta_ref[1:2].astype(jnp.int32), experts, back_ref)
    tokens = mid_ref.shape[0]
    squares = jnp.zeros((tokens, 1), F32)
    products = jnp.zeros((tokens, 1), F32)
    for q in range(QUARTERS):
        cols = quarter(q, width)
        mid = mid_ref[:, cols].astype(F32)
        value = gain_ref[:, cols] * rows_of(q)
        amount[:, cols] = value
        squares += jnp.sum(mid * mid, axis=-1, keepdims=True)
        products += jnp.sum(mid * value, axis=-1, keepdims=True)
    scale = lax.rsqrt(squares / features + EPS)
    factor = scale * scale * scale * (products / features)
    for q in range(QUARTERS):
        cols = quarter(q, width)
        out_ref[:, cols] = (
            grad_ref[:, cols].astype(F32)
            + scale * amount[:, cols]
            - mid_ref[:, cols].astype(F32) * factor
        ).astype(BF)


def place():
    section, index = lax.axis_index("section"), lax.axis_index("expert")
    return section, index // (2 * NX), (index // 2) % NX, index % 2


def device(section, z, x, core):
    return (section, (z * NX + x) * 2 + core)


def far_first(planes):
    near = sorted(range(1, planes), key=lambda d: -min(d, planes - d))
    return near


def near_first(planes):
    return sorted(range(1, planes), key=lambda d: min(d, planes - d))


def greet(targets):
    barrier = pltpu.get_barrier_semaphore()
    for target in targets:
        pl.semaphore_signal(barrier, inc=1, device_id=target, device_id_type=MESH)
    pl.semaphore_wait(barrier, len(targets))


def remote(src, dst, send, recv, target):
    return pltpu.make_async_remote_copy(
        src_ref=src, dst_ref=dst, send_sem=send, recv_sem=recv,
        device_id=target, device_id_type=MESH,
    )


class Dispatch:
    def __init__(self, send_ref, zbuf, out_ref, zsend, zrecv, xsend, xrecv, local):
        self.refs = (send_ref, zbuf, out_ref)
        self.sems = (zsend, zrecv, xsend, xrecv, local)
        self.planes = send_ref.shape[0]
        self.started = []

    def start(self):
        send_ref, zbuf, _ = self.refs
        zsend, zrecv, _, _, local = self.sems
        s, z, x, c = place()
        for d in far_first(self.planes):
            to = (z + d) % self.planes
            copy = remote(
                send_ref.at[to], zbuf.at[z], zsend.at[d], zrecv.at[z], device(s, to, x, c)
            )
            copy.start()
            self.started.append(copy)
        self.own = pltpu.make_async_copy(send_ref.at[z], zbuf.at[z], local.at[self.planes])
        self.own.start()

    def forward(self, d):
        send_ref, zbuf, out_ref = self.refs
        zsend, zrecv, xsend, xrecv, local = self.sems
        s, z, x, c = place()
        origin = (z + d) % self.planes
        if d == 0:
            self.own.wait()
        else:
            remote(
                send_ref.at[origin], zbuf.at[origin], zsend.at[d], zrecv.at[origin],
                device(s, origin, x, c),
            ).wait_recv()
        for dx in (2, 1, 3):
            to = (x + dx) % NX
            copy = remote(
                zbuf.at[origin, pl.ds(4 * (to // 2), 5)], out_ref.at[x, origin],
                xsend.at[dx - 1, d], xrecv.at[x, origin], device(s, z, to, c),
            )
            copy.start()
            self.started.append(copy)
        mine = pltpu.make_async_copy(
            zbuf.at[origin, pl.ds(4 * (x // 2), 5)], out_ref.at[x, origin], local.at[d]
        )
        mine.start()
        self.started.append(mine)

    def finish(self):
        send_ref, zbuf, out_ref = self.refs
        zsend, zrecv, xsend, xrecv, local = self.sems
        s, z, x, c = place()
        for d in range(self.planes):
            origin = (z + d) % self.planes
            for dx in range(1, NX):
                source = (x + dx) % NX
                remote(
                    zbuf.at[origin, pl.ds(0, 5)], out_ref.at[source, origin],
                    xsend.at[dx - 1, d], xrecv.at[source, origin], device(s, z, source, c),
                ).wait_recv()
        for copy in self.started:
            if hasattr(copy, "wait_send") and copy.is_remote:
                copy.wait_send()
            else:
                copy.wait()

    @staticmethod
    def scratch(planes, width):
        dma = pltpu.SemaphoreType.DMA
        return [
            pltpu.VMEM((planes, 9, 8, width), BF),
            dma((planes,)), dma((planes,)), dma((NX - 1, planes)), dma((NX, planes)),
            dma((planes + 1,)),
        ]


class Return:
    def __init__(self, part_ref, pbuf, stage, out_ref, xsend, xrecv, zsend, zrecv, local, by):
        self.refs = (part_ref, pbuf, stage, out_ref)
        self.sems = (xsend, xrecv, zsend, zrecv, local)
        self.planes = part_ref.shape[1]
        self.by = by
        self.started = []

    def order(self):
        return far_first(self.planes) + [0]

    def start(self):
        part_ref, pbuf, _, _ = self.refs
        xsend, xrecv, _, _, local = self.sems
        s, z, x, c = place()
        self.own = {}
        for d in self.order():
            origin = (z + d) % self.planes
            for dx in (2, 1, 3):
                to = (x + dx) % NX
                copy = remote(
                    part_ref.at[to, origin], pbuf.at[x, origin],
                    xsend.at[dx - 1, d], xrecv.at[x, origin], device(s, z, to, c),
                )
                copy.start()
                self.started.append(copy)
            self.own[d] = pltpu.make_async_copy(
                part_ref.at[x, origin], pbuf.at[x, origin], local.at[d]
            )
            self.own[d].start()

    def forward(self, d):
        part_ref, pbuf, stage, out_ref = self.refs
        xsend, xrecv, zsend, zrecv, local = self.sems
        s, z, x, c = place()
        origin = (z + d) % self.planes
        self.own[d].wait()
        for dx in range(1, NX):
            source = (x + dx) % NX
            remote(
                part_ref.at[source, origin], pbuf.at[source, origin],
                xsend.at[dx - 1, d], xrecv.at[source, origin], device(s, z, source, c),
            ).wait_recv()
        for k in range(4):
            stage[origin, k] = (
                pbuf[0, origin, k].astype(F32) + pbuf[1, origin, k].astype(F32)
            ).astype(BF)
            stage[origin, 5 + k] = (
                pbuf[2, origin, 1 + k].astype(F32) + pbuf[3, origin, 1 + k].astype(F32)
            ).astype(BF)
        stage[origin, 4] = (
            (pbuf[0, origin, 4].astype(F32) + pbuf[1, origin, 4].astype(F32))
            + (pbuf[2, origin, 0].astype(F32) + pbuf[3, origin, 0].astype(F32))
        ).astype(BF)
        sections = lax.axis_size("section")
        copy = remote(
            stage.at[origin], out_ref.at[z], zsend.at[d], zrecv.at[z],
            device((s + self.by + sections) % sections, origin, x, c),
        )
        copy.start()
        self.started.append(copy)

    def finish(self):
        part_ref, pbuf, stage, out_ref = self.refs
        xsend, xrecv, zsend, zrecv, local = self.sems
        s, z, x, c = place()
        sections = lax.axis_size("section")
        for d in range(self.planes):
            origin = (z + d) % self.planes
            remote(
                stage.at[origin], out_ref.at[origin], zsend.at[d], zrecv.at[origin],
                device((s - self.by + sections) % sections, origin, x, c),
            ).wait_recv()
        for copy in self.started:
            copy.wait_send()

    @staticmethod
    def scratch(planes, width):
        dma = pltpu.SemaphoreType.DMA
        return [
            pltpu.VMEM((NX, planes, 5, 8, width), BF),
            pltpu.VMEM((planes, 9, 8, width), BF),
            dma((NX - 1, planes)), dma((NX, planes)), dma((planes,)), dma((planes,)),
            dma((planes,)),
        ]


def row_peers(planes):
    s, z, x, c = place()
    peers = [device(s, (z + d) % planes, x, c) for d in range(1, planes)]
    return peers + [device(s, z, (x + d) % NX, c) for d in range(1, NX)]


def section_peers(planes, sections):
    s, z, x, c = place()
    return [
        device((s + by) % sections, (z + d) % planes, x, c)
        for by in (1, sections - 1) for d in range(planes)
    ]


def swap(refs, outs, send, recv, target):
    copies = []
    for i, (ref, out) in enumerate(zip(refs, outs)):
        copy = remote(ref, out, send.at[i], recv.at[i], target)
        copy.start()
        copies.append(copy)
    return copies


def kernel_a(
    rows_ref, grads_ref, wg, wu, wd, mid, grad, gain, meta,
    rows_out, grads_out, pg, pu, pd, mid_out, grad_out, gain_out, meta_out,
    *scratch,
):
    half = (len(scratch) - 2) // 2
    s, z, x, c = place()
    sections = lax.axis_size("section")
    planes = rows_ref.shape[0]
    before = device((s + sections - 1) % sections, z, x, c)
    after = device((s + 1) % sections, z, x, c)
    core = device(s, z, x, 1 - c)
    greet(row_peers(planes) + [before, after, core])
    send, recv = scratch[-2:]
    ones = Dispatch(rows_ref, scratch[0], rows_out, *scratch[1:half])
    twos = Dispatch(grads_ref, scratch[half], grads_out, *scratch[half + 1 : 2 * half])
    ones.start()
    twos.start()
    copies = swap((wg, wu, wd), (pg, pu, pd), send.at[0], recv.at[0], core)
    copies += swap(
        (mid, grad, gain, meta), (mid_out, grad_out, gain_out, meta_out),
        send.at[1], recv.at[1], before,
    )
    for one in (ones, twos):
        for d in [0] + near_first(planes):
            one.forward(d)
    ones.finish()
    twos.finish()
    for copy in copies:
        copy.wait()


def kernel_b(send_ref, part_ref, middle, meta, rows_out, back_out, middle_out, meta_out, *scratch):
    s, z, x, c = place()
    sections = lax.axis_size("section")
    planes = send_ref.shape[0]
    greet(row_peers(planes) + section_peers(planes, sections))
    front = Dispatch(send_ref, scratch[0], rows_out, *scratch[1:6])
    back = Return(part_ref, scratch[6], scratch[7], back_out, *scratch[8:13], -1)
    send, recv = scratch[-2:]
    front.start()
    back.start()
    copies = swap(
        (middle, meta), (middle_out, meta_out), send, recv,
        device((s + 1) % sections, z, x, c),
    )
    for d, b in zip([0] + near_first(planes), back.order()):
        back.forward(b)
        front.forward(d)
    front.finish()
    back.finish()
    for copy in copies:
        copy.wait()


def kernel_c(part_ref, back_out, *scratch):
    planes = part_ref.shape[1]
    s, z, x, c = place()
    sections = lax.axis_size("section")
    greet(row_peers(planes)[planes - 1 :] + section_peers(planes, sections))
    front = Return(part_ref, scratch[0], scratch[1], back_out, *scratch[2:7], 1)
    front.start()
    for d in front.order():
        front.forward(d)
    front.finish()


ANY = pl.BlockSpec(memory_space=pl.ANY)
VMEM = pl.BlockSpec(memory_space=pltpu.VMEM)
SMEM = pl.BlockSpec(memory_space=pltpu.SMEM)


def like(*arrays):
    return [jax.ShapeDtypeStruct(a.shape, a.dtype) for a in arrays]


def speak(kernel, number, out_shape, scratch, *args):
    return pl.pallas_call(
        kernel,
        out_shape=out_shape,
        in_specs=[ANY] * len(args),
        out_specs=[ANY] * len(out_shape),
        scratch_shapes=scratch,
        compiler_params=pltpu.CompilerParams(
            collective_id=number, has_side_effects=True, vmem_limit_bytes=24 << 20
        ),
    )(*args)


def compute(kernel, out_shape, *args, specs=None, scratch=(), mib=48):
    return pl.pallas_call(
        kernel,
        out_shape=out_shape,
        in_specs=specs or [VMEM] * len(args),
        out_specs=jax.tree.map(lambda _: VMEM, out_shape),
        scratch_shapes=list(scratch),
        compiler_params=pltpu.CompilerParams(vmem_limit_bytes=mib << 20),
    )(*args)


def shards(
    front_input, queries, keys_values, selected_blocks, front_route, front_gate,
    back_middle, back_grad, back_route, back_gate, norm_gain, gate_slice, up_slice, down_slice,
):
    tokens, features = front_input.shape[1:]
    planes = lax.axis_size("expert") // (2 * NX)
    width = features // QUARTERS
    wg, wu, wd = gate_slice[0, 0], up_slice[0, 0], down_slice[0, 0]
    mid, grad, entry = back_middle[0], back_grad[0], front_input[0]
    f_route = front_route.reshape(1, tokens)
    b_route = back_route.reshape(1, tokens)
    f_meta = jnp.concatenate(
        [front_gate.reshape(1, tokens), f_route.astype(F32), jnp.zeros((6, tokens), F32)]
    )
    b_meta = jnp.concatenate(
        [back_gate.reshape(1, tokens), b_route.astype(F32), jnp.zeros((6, tokens), F32)]
    )
    kv = keys_values[0].reshape(tokens, 2 * KV_HEADS, HEAD_DIM).transpose(1, 0, 2)
    kv = jnp.pad(kv, ((0, 0), (0, 0), (0, 128 - HEAD_DIM)))
    gathered = lax.all_gather(kv, "expert")
    index = lax.axis_index("expert")
    half = ((index // 4) % 2).astype(jnp.int32).reshape(1)
    message = jax.ShapeDtypeStruct((planes, 9, 8, width), BF)
    arrived = jax.ShapeDtypeStruct((NX, planes, 5, 8, width), BF)
    flat = jax.ShapeDtypeStruct((NX * planes, 5, 8, width), BF)
    dma = pltpu.SemaphoreType.DMA

    with jax.named_scope("back_pack"):
        back_rows, back_grads = compute(
            back_pack_kernel, [message, message], mid, grad, norm_gain,
            back_gate.reshape(1, tokens), b_route,
        )
    with jax.named_scope("exchange_a"):
        (rows_in, grads_in, pg, pu, pd, mid_in, grad_in, gain_in, b_meta_in) = speak(
            kernel_a, 0, [arrived, arrived] + like(wg, wu, wd, mid, grad, norm_gain, b_meta),
            Dispatch.scratch(planes, width) * 2 + [dma((2, 4)), dma((2, 4))],
            back_rows, back_grads, wg, wu, wd, mid, grad, norm_gain, b_meta,
        )
    with jax.named_scope("attention"):
        blocks = tokens // BLK
        picks = jnp.concatenate(
            [selected_blocks.reshape(-1), (index * blocks).astype(jnp.int32).reshape(1)]
        )
        middle, front_rows = compute(
            attention_kernel,
            [jax.ShapeDtypeStruct((tokens, features), BF), message],
            picks, queries[0], gathered, entry, norm_gain, f_route,
            specs=[SMEM, VMEM, ANY, VMEM, VMEM, VMEM],
            scratch=[
                pltpu.VMEM((blocks * KV_HEADS, SEL * BLK, 128), BF),
                pltpu.VMEM((blocks * KV_HEADS, SEL * BLK, 128), BF),
                pltpu.VMEM((tokens, features), F32),
                dma((2, blocks * KV_HEADS * SEL)),
            ],
        )
    weights = (wg, wu, wd, pg, pu, pd)
    with jax.named_scope("backward_experts"):
        back_part = compute(
            backward_kernel, flat, half, rows_in.reshape(flat.shape),
            grads_in.reshape(flat.shape), *weights, specs=[SMEM] + [VMEM] * 8,
        )
    with jax.named_scope("exchange_b"):
        rows_in, back_out, middle_in, f_meta_in = speak(
            kernel_b, 1, [arrived, message] + like(middle, f_meta),
            Dispatch.scratch(planes, width) + Return.scratch(planes, width) + [dma((2,)), dma((2,))],
            front_rows, back_part.reshape(arrived.shape), middle, f_meta,
        )
    with jax.named_scope("forward_experts"):
        front_part = compute(
            forward_kernel, flat, half, rows_in.reshape(flat.shape), *weights,
            specs=[SMEM] + [VMEM] * 7,
        )
    with jax.named_scope("back_last"):
        back_output = compute(
            back_last_kernel, jax.ShapeDtypeStruct((tokens, features), BF),
            mid_in, grad_in, gain_in, back_out, b_meta_in,
            scratch=[pltpu.VMEM((tokens, features), F32)],
        )
    with jax.named_scope("exchange_c"):
        (front_out,) = speak(
            kernel_c, 2, [message], Return.scratch(planes, width),
            front_part.reshape(arrived.shape),
        )
    with jax.named_scope("front_last"):
        front_output = compute(
            front_last_kernel, jax.ShapeDtypeStruct((tokens, features), BF),
            middle_in, front_out, f_meta_in,
        )
    return (front_output[None], back_output[None])


def solution(mesh):
    rows = P("section", "expert", None)
    wide = P("section", "expert", None, None)
    return jax.shard_map(
        shards,
        mesh=mesh,
        in_specs=(rows, rows, rows, wide, rows, rows, rows, rows, rows, rows,
                  P("section", None), wide, wide, wide),
        out_specs=(rows, rows),
        check_vma=False,
    )
```

time: 975 us -> 279 us (0.29)
  waiting for transfers between devices: 689 us -> 0.02 us
  Pallas kernels: 0 us -> 234 us
  local copies, waits for them, and re-layouts: 156 us -> 25.8 us
  starting transfers between devices: 43.2 us -> 0.04 us
  other arithmetic: 36 us -> 1.46 us
  matrix products: 27.6 us -> 0 us
    all_to_all x5 -> x0, waiting for transfers between devices: 666 us -> none  [the longest x1 177 us: shards(): lax.all_to_all(back_send_rows, 'expert', split_axis=0, concat_axis=0, til...]
    pallas_call x0 -> x9, Pallas kernels: none -> 234 us  [the longest x3 196 us: speak(): pl.pallas_call(kernel, out_shape=out_shape, in_specs=[ANY] * len(args), o...]
    reshape x13 -> x1, local copies, waits for them, and re-layouts: 106 us -> 0.77 us  [shards(): selected_blocks.reshape(-1)]
    all_to_all x5 -> x0, starting transfers between devices: 38.1 us -> none  [the longest x1 11.9 us: shards(): lax.all_to_all(back_send_rows, 'expert', split_axis=0, concat_axis=0, til...]
    dot_general x8 -> x0, matrix products: 27.6 us -> none  [the longest x1 9.2 us: slice_forward(): jnp.dot(hidden, w_down, preferred_element_type=jnp.float32)]
    gather x4 -> x0, local copies, waits for them, and re-layouts: 23.2 us -> none  [the longest x2 15.2 us: unpack_rows(): picked = grid[destination // capacity, :, destination % capacity]]
    ppermute x2 -> x0, waiting for transfers between devices: 21.9 us -> none  [passed_along(): lax.ppermute(array, axis, [(i, (i + by) % length) for i in range(length)])]
    unnamed x28 -> x63, local copies, waits for them, and re-layouts: 5.65 us -> 24.2 us
  transfers between devices with their start and end apart: 8 -> 1, of which waited for: 6 -> 0; matrix products, arithmetic and copies ran while one was open for 22% -> 1% of each run, Pallas kernels for 0% -> 41%
where the time goes in v1:
time: 279 us; the launch traced here: 276 us
  Pallas kernels  234 us (84%)
  local copies, waits for them, and re-layouts  25.8 us (9%)
  between operations  14.2 us (5%)
    pallas_call x3, Pallas kernels, speak(): pl.pallas_call(kernel, out_shape=out_shape, in_specs=[ANY] * len(args), o...  196 us
    pallas_call x6, Pallas kernels, compute(): pl.pallas_call(kernel, out_shape=out_shape, in_specs=specs or [VMEM] * le...  38.2 us
    unnamed x63, local copies, waits for them, and re-layouts  24.2 us
  transfers between devices with their start and end apart: 1, of which 0 were waited for; matrix products, arithmetic and copies ran while one was open for 1% of the time, Pallas kernels for 41%

profile of v1, /device:TPU:34, one launch (start us, length us, event | category | flops | bytes accessed | tf_op | source)
XLA Modules:
  0.0 276.0 jit_solution(17206405127144941891)
XLA Ops:
  7.2 1.1 copy.18
  8.4 0.7 pad.4.clone
  9.1 0.8 reshape.65
  10.0 1.2 copy-done.12
  11.1 1.2 copy-done.14
  12.3 0.7 copy-done.25
  14.3 1.2 back_pack.1
  15.5 0.7 bitcast_convert_fusion
  16.2 0.7 maximum_maximum_fusion.1
  16.9 1.5 copy-done.1
  18.4 1.5 copy-done.4
  19.9 1.2 copy-done.13
  21.1 1.2 copy-done.15
  22.3 0.7 copy-done.26
  23.0 99.7 %exchange_a.1 = (bf16[4,8,5,8,896]{4,3,2,1,0:T(8,128)(2,1)S(1)}, bf16[4,8,5,8,896]{4,3,2,1,0:T(8,128)(2,1)S(1)}, bf16[3584,256]{1,0:T(8,128)(2,1)S(1)}, bf16[358...) custom-call(bf16[8,9,8,896]{3,2,1,0:T(8,128)(2,1)S(1)} %get-tuple-el, ...), custom_call_target="tpu_custom_call" | custom-call | tf_op jit(solution)/shard_map/exchange_a/pallas_call | solution.py:605
  122.7 1.2 copy-done.9
  123.9 1.3 copy-done.10
  125.2 1.2 copy-done.11
  126.4 1.5 copy-done.16
  127.9 1.3 copy-done.17
  129.3 0.9 copy-done.21
  130.2 0.9 copy-done.23
  131.2 12.9 %backward_experts.1 = bf16[32,5,8,896]{3,2,1,0:T(8,128)(2,1)} custom-call(s32[1]{0:T(128)} %bitcast.7.h_ref, bf16[32,5,8,896]{3,2,1,0:T(8,128)(2,1)} %bitcast.41, bf16[32,5,8,896]{3,2,1,0:T(8,128)(2,1)} %bitcast.42, bf16[3584,256]{1,0:T(8,128)(2,1)S(1)} %bitcast.27, bf16[3584,256]{1,0:T(8,128)(2,1)S(1)} %bitcast.30, bf16[256,3584]{1,0:T(8,128)(2,1)S(1)} %bitcast.33, ...), custom_call_target="tpu_custom_call" | custom-call | tf_op jit(solution)/shard_map/backward_experts/pallas_call | solution.py:618
  144.2 1.2 copy-done.20
  145.4 10.3 %attention.1 = (bf16[128,3584]{1,0:T(8,128)(2,1)S(1)}, bf16[8,9,8,896]{3,2,1,0:T(8,128)(2,1)S(1)}) custom-call(s32[17]{0:T(128)S(1)} %pad_add_fusion.sel_ref, bf16[128,3584]{1,0:T(8,128)(2,1)S(1)} %bitcast.44, bf16[64,4,128,128]{3,2,1,0:T(8,128)(2,1)} %bitcast.50, bf16[128,3584]{1,0:T(8,128)(2,1)S(1)} %bitcast.45, f32[1,3584]{1,0:T(1,128)S(1)} %copy-done.27, ...), custom_call_target="tpu_custom_call" | custom-call | tf_op jit(solution)/shard_map/attention/pallas_call | solution.py:618
  155.7 57.5 %exchange_b.1 = (bf16[4,8,5,8,896]{4,3,2,1,0:T(8,128)(2,1)S(1)}, bf16[8,9,8,896]{3,2,1,0:T(8,128)(2,1)S(1)}, bf16[128,3584]{1,0:T(8,128)(2,1)S(1)}, f32[8,128]{1,0:T(8,128)S(1)}) custom-call(bf16[8,9,8,896]{3,2,1,0:T(8,128)(2,1)S(1)} %get-tuple-element.19.send_ref, bf16[4,8,5,8,896]{4,3,2,1,0:T(8,128)(2,1)S(1)} %bitcast.35, ...), custom_call_target="tpu_custom_call" | custom-call | tf_op jit(solution)/shard_map/exchange_b/pallas_call | solution.py:605
  213.2 1.4 copy-done.18
  214.6 9.8 %forward_experts.1 = bf16[32,5,8,896]{3,2,1,0:T(8,128)(2,1)} custom-call(s32[1]{0:T(128)} %bitcast.7.h_ref, bf16[32,5,8,896]{3,2,1,0:T(8,128)(2,1)} %bitcast.43, bf16[3584,256]{1,0:T(8,128)(2,1)S(1)} %bitcast.28, bf16[3584,256]{1,0:T(8,128)(2,1)S(1)} %bitcast.31, bf16[256,3584]{1,0:T(8,128)(2,1)S(1)} %bitcast.34, bf16[3584,256]{1,0:T(8,128)(2,1)} %copy-done.9, ...), custom_call_target="tpu_custom_call" | custom-call | tf_op jit(solution)/shard_map/forward_experts/pallas_call | solution.py:618
  224.4 1.6 copy-done.8
  226.0 39.0 %exchange_c.1.back_ref = bf16[8,9,8,896]{3,2,1,0:T(8,128)(2,1)S(1)} custom-call(bf16[4,8,5,8,896]{4,3,2,1,0:T(8,128)(2,1)S(1)} %bitcast.36), custom_call_target="tpu_custom_call" | custom-call | tf_op jit(solution)/shard_map/exchange_c/pallas_call | solution.py:605
  265.1 1.8 front_last.1
  266.9 2.2 back_last.1
  (50 shorter events, 1.6 us)
Async XLA Ops:
  7.2 9.8 %copy-start = (bf16[1,1,3584,256]{3,2,1,0:T(8,128)(2,1)S(1)}, bf16[1,1,3584,256]{3,2,1,0:T(8,128)(2,1)}, u32[]{:S(2)}) copy-start(bf16[1,1,3584,256]{3,2,1,0:T(8,128)(2,1)} %param.25) | copy-start | bytes 5505028
  7.2 137.0 %all-gather.3.cloned.1.call-start = ((), (), s32[]{:S(2)}) async-start(), calls=%async_computation | async-start | bytes 8519680 | tf_op jit(solution)/shard_map/all_gather | solution.py:647
  10.0 1.2 copy-start.12
  11.1 1.2 copy-start.14
  12.3 0.7 copy-start.25
  13.0 0.7 copy-start.29
  13.7 0.7 copy-start.30
  16.9 1.5 copy-start.1
  18.4 1.5 copy-start.4
  19.9 1.2 copy-start.13
  21.1 1.2 copy-start.15
  22.3 0.7 copy-start.26
  23.0 108.1 %copy-start.2 = (bf16[1,1,3584,256]{3,2,1,0:T(8,128)(2,1)S(1)}, bf16[1,1,3584,256]{3,2,1,0:T(8,128)(2,1)}, u32[]{:S(2)}) copy-start(bf16[1,1,3584,256]{3,2,1,0:T(8,128)(2,1)} %param.26) | copy-start | bytes 5505028
  23.0 108.1 %copy-start.5 = (bf16[1,1,256,3584]{3,2,1,0:T(8,128)(2,1)S(1)}, bf16[1,1,256,3584]{3,2,1,0:T(8,128)(2,1)}, u32[]{:S(2)}) copy-start(bf16[1,1,256,3584]{3,2,1,0:T(8,128)(2,1)} %param.27) | copy-start | bytes 5505028
  122.7 1.2 copy-start.9
  123.9 1.3 copy-start.10
  125.2 1.2 copy-start.11
  126.4 1.5 copy-start.16
  127.9 1.3 copy-start.17
  129.3 0.9 copy-start.21
  130.2 0.9 copy-start.23
  131.1 13.0 %copy-start.19 = (bf16[1,128,3584]{2,1,0:T(8,128)(2,1)S(1)}, bf16[1,128,3584]{2,1,0:T(8,128)(2,1)}, u32[]{:S(2)}) copy-start(bf16[1,128,3584]{2,1,0:T(8,128)(2,1)} %param.15) | copy-start | bytes 2752516
  131.1 13.0 %copy-start.27 = (f32[1,3584]{1,0:T(1,128)S(1)}, f32[1,3584]{1,0:T(1,128)}, u32[]{:S(2)}) copy-start(f32[1,3584]{1,0:T(1,128)} %gain.1) | copy-start | bytes 43012
  131.1 13.0 %copy-start.28 = (s32[1,128,1]{1,2,0:T(1,128)S(1)}, s32[1,128,1]{1,2,0:T(1,128)}, u32[]{:S(2)}) copy-start(s32[1,128,1]{1,2,0:T(1,128)} %param.18) | copy-start | bytes 1540
  144.2 1.2 copy-start.20
  145.4 10.3 %copy-start.7 = (bf16[32,5,8,896]{3,2,1,0:T(8,128)(2,1)S(1)}, bf16[32,5,8,896]{3,2,1,0:T(8,128)(2,1)}, u32[]{:S(2)}) copy-start(bf16[32,5,8,896]{3,2,1,0:T(8,128)(2,1)} %backward_experts.1) | copy-start | bytes 6881284
  155.7 58.9 %copy-start.3 = (bf16[1,1,3584,256]{3,2,1,0:T(8,128)(2,1)S(1)}, bf16[1,1,3584,256]{3,2,1,0:T(8,128)(2,1)}, u32[]{:S(2)}) copy-start(bf16[1,1,3584,256]{3,2,1,0:T(8,128)(2,1)} %param.26) | copy-start | bytes 5505028
  155.7 58.9 %copy-start.6 = (bf16[1,1,256,3584]{3,2,1,0:T(8,128)(2,1)S(1)}, bf16[1,1,256,3584]{3,2,1,0:T(8,128)(2,1)}, u32[]{:S(2)}) copy-start(bf16[1,1,256,3584]{3,2,1,0:T(8,128)(2,1)} %param.27) | copy-start | bytes 5505028
  213.2 1.4 copy-start.18
  224.4 1.6 copy-start.8
  226.0 40.8 %copy-start.22 = (bf16[128,3584]{1,0:T(8,128)(2,1)S(1)}, bf16[128,3584]{1,0:T(8,128)(2,1)}, u32[]{:S(2)}) copy-start(bf16[128,3584]{1,0:T(8,128)(2,1)} %copy-done.21) | copy-start | bytes 2752516
  226.0 40.9 %copy-start.24 = (bf16[128,3584]{1,0:T(8,128)(2,1)S(1)}, bf16[128,3584]{1,0:T(8,128)(2,1)}, u32[]{:S(2)}) copy-start(bf16[128,3584]{1,0:T(8,128)(2,1)} %copy-done.23) | copy-start | bytes 2752516
Sparse Core Ops, SparseCore 0:
  11.4 117.2 all-gather.2

commit v2 on v1

v2 whole, which is shorter than its diff:
```python
import jax
import jax.numpy as jnp
from jax import lax
from jax.experimental import pallas as pl
from jax.experimental.pallas import tpu as pltpu
from jax.sharding import PartitionSpec as P

HEADS = 32
HEAD_DIM = 112
KV_HEADS = 2
GROUPS = HEADS // KV_HEADS
BLK = 64
SEL = 4
QUARTERS = 4
NX = 4
EPS = 1e-06
NEG = -1e30
MESH = pl.DeviceIdType.MESH
BF = jnp.bfloat16
F32 = jnp.float32


def iota(shape, dim):
    return lax.broadcasted_iota(jnp.int32, shape, dim)


def slot_row(route, experts):
    tokens = route.shape[1]
    onehot = jnp.where(iota((experts, tokens), 0) == route, 1.0, 0.0)
    earlier = jnp.where(iota((tokens, tokens), 0) < iota((tokens, tokens), 1), 1.0, 0.0)
    before = jnp.dot(onehot.astype(BF), earlier.astype(BF), preferred_element_type=F32)
    return jnp.sum(before * onehot, axis=0, keepdims=True).astype(jnp.int32)


def main_onehot(route, slot, experts):
    place = jnp.where(slot < 8, route * 8 + slot, -1)
    return jnp.where(iota((experts * 8, route.shape[1]), 0) == place, 1.0, 0.0)


def tail_onehot(route, slot, experts, quarter):
    place = jnp.where(slot >= 8, route * 4 + quarter, -1)
    return jnp.where(iota((experts * 4, route.shape[1]), 0) == place, 1.0, 0.0)


def pack(route, experts, rows_of, send_ref):
    slot = slot_row(route, experts)
    main = main_onehot(route, slot, experts).astype(BF)
    planes = experts // 2
    tail = None
    for q in range(QUARTERS):
        rows = rows_of(q)
        width = rows.shape[1]
        sorted_rows = jnp.dot(main, rows, preferred_element_type=F32).reshape(planes, 2, 8, width)
        send_ref[:, q] = sorted_rows[:, 0].astype(BF)
        send_ref[:, 5 + q] = sorted_rows[:, 1].astype(BF)
        last = jnp.dot(
            tail_onehot(route, slot, experts, q).astype(BF), rows, preferred_element_type=F32
        )
        tail = last if tail is None else tail + last
    send_ref[:, 4] = tail.reshape(planes, 8, width).astype(BF)


def unpack(route, experts, back_ref):
    slot = slot_row(route, experts)
    main = main_onehot(route, slot, experts).T.astype(BF)
    planes = experts // 2
    width = back_ref.shape[3]

    def rows_of(q):
        first = back_ref[:, q].astype(F32)
        second = back_ref[:, 5 + q].astype(F32)
        both = jnp.stack([first, second], axis=1).reshape(experts * 8, width).astype(BF)
        last = back_ref[:, 4].astype(F32).reshape(planes * 8, width).astype(BF)
        tail = tail_onehot(route, slot, experts, q).T.astype(BF)
        return jnp.dot(main, both, preferred_element_type=F32) + jnp.dot(
            tail, last, preferred_element_type=F32
        )

    return rows_of


def quarter(q, width):
    return slice(q * width, (q + 1) * width)


def normed_rows(ref, gain_ref, width):
    tokens, features = ref.shape
    squares = jnp.zeros((tokens, 1), F32)
    for q in range(QUARTERS):
        part = ref[:, quarter(q, width)].astype(F32)
        squares += jnp.sum(part * part, axis=-1, keepdims=True)
    scale = lax.rsqrt(squares / features + EPS)

    def rows_of(q):
        cols = quarter(q, width)
        return (ref[:, cols].astype(F32) * scale * gain_ref[:, cols]).astype(BF)

    return rows_of


def as_column(row):
    count = row.shape[1]
    return jnp.broadcast_to(row, (count, count)).T[:, 0:1]


def attend(pair, first, sel_ref, query_ref, kv_ref, total):
    b, h = pair // KV_HEADS, pair % KV_HEADS
    keys = SEL * BLK
    blocks = query_ref.shape[0] // BLK
    token_rows = slice(b * BLK, (b + 1) * BLK)
    chosen = [sel_ref[b, h, k] for k in range(SEL)]
    held = [[], []]
    for k in range(SEL):
        owner = chosen[k] // blocks
        spot = (owner % 2, owner // (2 * NX), (owner // 2) % NX)
        for w in range(2):
            held[w].append(kv_ref[h][(*spot, w)])
    lane = iota((2 * BLK, keys), 1)
    key_pos = lane % BLK
    at, to = iota((blocks * BLK, keys), 0), iota((blocks * BLK, keys), 1)
    picks = []
    for k in range(SEL):
        key_pos = key_pos + jnp.where(lane // BLK == k, chosen[k] * BLK, 0)
        inside = (at == to % BLK + (chosen[k] % blocks) * BLK) & (to // BLK == k)
        picks.append(jnp.where(inside, 1.0, 0.0).astype(BF))
    allowed = key_pos <= (first + b) * BLK + iota((2 * BLK, keys), 0) % BLK

    def selected(pieces):
        out = None
        for piece, pick in zip(pieces, picks):
            more = jnp.dot(piece, pick, preferred_element_type=F32)
            out = more if out is None else out + more
        return out.astype(BF)

    key_cols, value_cols = selected(held[0]), selected(held[1])
    for g in range(GROUPS // 2):
        offset = (HEAD_DIM * g) % 128
        window = 128 if offset + HEAD_DIM <= 128 else 256
        shift = jnp.where(
            iota((window, HEAD_DIM), 0) == iota((window, HEAD_DIM), 1) + offset, 1.0, 0.0
        ).astype(BF)
        key_moved = jnp.dot(shift, key_cols, preferred_element_type=F32).astype(BF)
        value_moved = jnp.dot(shift, value_cols, preferred_element_type=F32).astype(BF)
        starts = [
            HEAD_DIM * (h * GROUPS + g + half * (GROUPS // 2)) // 128 * 128 for half in range(2)
        ]
        query = jnp.concatenate([query_ref[token_rows, s : s + window] for s in starts], axis=0)
        scores = jnp.dot(query, key_moved, preferred_element_type=F32) * HEAD_DIM ** (-0.5)
        scores = jnp.where(allowed, scores, NEG)
        exp_scores = jnp.exp(scores - jnp.max(scores, axis=-1, keepdims=True))
        weights = exp_scores / jnp.sum(exp_scores, axis=-1, keepdims=True)
        mixed = lax.dot_general(
            weights.astype(BF), value_moved, (((1,), (1,)), ((), ())), preferred_element_type=F32
        )
        for half, s in enumerate(starts):
            total[token_rows, s : s + window] += mixed[half * BLK : (half + 1) * BLK]

def tail_select(count, q):
    row, col = iota((count, count * 4), 0), iota((count, count * 4), 1)
    return jnp.where(col == row * 4 + q, 1.0, 0.0).astype(BF)


def rows_for_expert(main_ref, tail_ref, q):
    count, width = main_ref.shape[0], main_ref.shape[3]
    main = main_ref[:, q].astype(F32).reshape(count * 8, width).astype(BF)
    last = tail_ref[...].astype(F32).reshape(count * 4, width).astype(BF)
    tail = jnp.dot(tail_select(count, q), last, preferred_element_type=F32).astype(BF)
    return jnp.concatenate([main, tail], axis=0)


def store_for_source(main_ref, q, value, tail_total):
    count, width = main_ref.shape[0], main_ref.shape[3]
    main_ref[:, q] = value[: count * 8].reshape(count, 8, width).astype(BF)
    spread = lax.dot_general(
        tail_select(count, q), value[count * 8 :].astype(BF),
        (((0,), (0,)), ((), ())), preferred_element_type=F32,
    )
    return spread if tail_total is None else tail_total + spread


def forward_experts(recv, own, other, out):
    width = recv[0].shape[3]
    sides = (own, other)
    gates, ups = [None, None], [None, None]
    for q in range(QUARTERS):
        rows = rows_for_expert(*recv, q)
        part = quarter(q, width)
        for i, (g, u, _) in enumerate(sides):
            gate = jnp.dot(rows, g[part], preferred_element_type=F32)
            up = jnp.dot(rows, u[part], preferred_element_type=F32)
            gates[i] = gate if gates[i] is None else gates[i] + gate
            ups[i] = up if ups[i] is None else ups[i] + up
    hidden = [(v / (1.0 + jnp.exp(-v)) * u).astype(BF) for v, u in zip(gates, ups)]
    tail = None
    for q in range(QUARTERS):
        part = quarter(q, width)
        value = jnp.dot(hidden[0], own[2][:, part], preferred_element_type=F32) + jnp.dot(
            hidden[1], other[2][:, part], preferred_element_type=F32
        )
        tail = store_for_source(out[0], q, value, tail)
    out[1][...] = tail.reshape(out[1].shape).astype(BF)


def backward_experts(recv, recv_grad, own, other, out):
    width = recv[0].shape[3]
    last = (((1,), (1,)), ((), ()))
    sides = (own, other)
    gates, ups, downs = [None, None], [None, None], [None, None]
    for q in range(QUARTERS):
        rows = rows_for_expert(*recv, q)
        grads = rows_for_expert(*recv_grad, q)
        part = quarter(q, width)
        for i, (g, u, d) in enumerate(sides):
            gate = jnp.dot(rows, g[part], preferred_element_type=F32)
            up = jnp.dot(rows, u[part], preferred_element_type=F32)
            down = lax.dot_general(grads, d[:, part], last, preferred_element_type=F32)
            gates[i] = gate if gates[i] is None else gates[i] + gate
            ups[i] = up if ups[i] is None else ups[i] + up
            downs[i] = down if downs[i] is None else downs[i] + down
    gate_grads, up_grads = [], []
    for gate, up, down in zip(gates, ups, downs):
        sigmoid = 1.0 / (1.0 + jnp.exp(-gate))
        gate_grads.append((down * up * (sigmoid * (1.0 + gate * (1.0 - sigmoid)))).astype(BF))
        up_grads.append((down * (gate * sigmoid)).astype(BF))
    tail = None
    for q in range(QUARTERS):
        part = quarter(q, width)
        value = None
        for i, (g, u, _) in enumerate(sides):
            more = lax.dot_general(
                gate_grads[i], g[part], last, preferred_element_type=F32
            ) + lax.dot_general(up_grads[i], u[part], last, preferred_element_type=F32)
            value = more if value is None else value + more
        tail = store_for_source(out[0], q, value, tail)
    out[1][...] = tail.reshape(out[1].shape).astype(BF)


def front_last_kernel(
    middle_hbm, back_hbm, meta_hbm, done_hbm, out_hbm, done_out,
    middle_ref, back_ref, meta_ref, out_ref, done_ref, sem,
):
    width = back_ref.shape[3]
    experts = back_ref.shape[0] * 2
    pairs = (
        (meta_hbm, meta_ref), (back_hbm, back_ref), (middle_hbm, middle_ref), (done_hbm, done_ref),
    )
    copies = [pltpu.make_async_copy(a, b, sem.at[i]) for i, (a, b) in enumerate(pairs)]
    for copy in copies:
        copy.start()
    for copy in copies:
        copy.wait()
    copies = [pltpu.make_async_copy(done_ref, done_out, sem.at[4])]
    copies[0].start()
    gate = as_column(meta_ref[0:1])
    rows_of = unpack(meta_ref[1:2].astype(jnp.int32), experts, back_ref)
    for q in range(QUARTERS):
        cols = quarter(q, width)
        out_ref[:, cols] = (middle_ref[:, cols].astype(F32) + gate * rows_of(q)).astype(BF)
        copy = pltpu.make_async_copy(out_ref.at[:, cols], out_hbm.at[:, cols], sem.at[5 + q])
        copy.start()
        copies.append(copy)
    for copy in copies:
        copy.wait()


def back_last(mid_ref, grad_ref, gain_ref, back_ref, meta_ref, out_ref, amount):
    experts = back_ref.shape[0] * 2
    width = back_ref.shape[3]
    tokens, features = mid_ref.shape
    rows_of = unpack(meta_ref[1:2].astype(jnp.int32), experts, back_ref)
    squares = jnp.zeros((tokens, 1), F32)
    products = jnp.zeros((tokens, 1), F32)
    for q in range(QUARTERS):
        cols = quarter(q, width)
        mid = mid_ref[:, cols].astype(F32)
        value = gain_ref[:, cols] * rows_of(q)
        amount[:, cols] = value
        squares += jnp.sum(mid * mid, axis=-1, keepdims=True)
        products += jnp.sum(mid * value, axis=-1, keepdims=True)
    scale = lax.rsqrt(squares / features + EPS)
    factor = scale * scale * scale * (products / features)
    for q in range(QUARTERS):
        cols = quarter(q, width)
        out_ref[:, cols] = (
            grad_ref[:, cols].astype(F32)
            + scale * amount[:, cols]
            - mid_ref[:, cols].astype(F32) * factor
        ).astype(BF)


def place():
    section, index = lax.axis_index("section"), lax.axis_index("expert")
    return section, index // (2 * NX), (index // 2) % NX, index % 2


def device(section, z, x, core):
    return (section, (z * NX + x) * 2 + core)


def far_first(planes):
    return sorted(range(1, planes), key=lambda d: -min(d, planes - d))


def stages_of(planes):
    return [sorted({d, planes - d}) for d in range(1, planes // 2 + 1)]


class Flow:
    def __init__(self, items, depth):
        self.unsent = list(items)
        self.waiting = []
        self.depth = depth

    def fill(self):
        while self.unsent and self.sent < self.depth:
            one, d = self.unsent.pop(0)
            one.send(d)
            self.waiting.append((one, d))
            self.sent += 1

    def open(self):
        self.sent = 0
        self.fill()

    def more(self, items):
        self.unsent += items
        self.fill()

    def left(self):
        return len(self.waiting) + len(self.unsent)

    def turn(self, count=1):
        for _ in range(count):
            one, d = self.waiting.pop(0)
            self.sent -= 1
            self.fill()
            one.forward(d)


def greet(targets):
    barrier = pltpu.get_barrier_semaphore()
    for target in targets:
        pl.semaphore_signal(barrier, inc=1, device_id=target, device_id_type=MESH)
    pl.semaphore_wait(barrier, len(targets))


def remote(src, dst, send, recv, target):
    return pltpu.make_async_remote_copy(
        src_ref=src, dst_ref=dst, send_sem=send, recv_sem=recv,
        device_id=target, device_id_type=MESH,
    )


def dma(*shape):
    return pltpu.SemaphoreType.DMA(shape)


class Gather:
    def __init__(self, kv, zsend, zrecv, xsend, xrecv, csend, crecv):
        self.kv = kv
        self.sems = (zsend, zrecv, xsend, xrecv, csend, crecv)
        self.planes = kv[0].shape[1]
        self.started = []

    def go(self, ref, send, recv, target):
        copy = remote(ref, ref, send, recv, target)
        copy.start()
        self.started.append(copy)

    def along_x(self, h, origin, d):
        _, _, xsend, xrecv, _, _ = self.sems
        s, z, x, c = place()
        for dx in (2, 1, 3):
            self.go(
                self.kv[h].at[c, origin, x], xsend.at[h, d, dx - 1], xrecv.at[h, origin, x],
                device(s, z, (x + dx) % NX, c),
            )

    def await_x(self, h, origin, d):
        _, _, xsend, xrecv, _, _ = self.sems
        s, z, x, c = place()
        for dx in (1, 3, 2):
            ref = self.kv[h].at[c, origin, (x + dx) % NX]
            remote(
                ref, ref, xsend.at[h, d, dx - 1], xrecv.at[h, origin, (x + dx) % NX],
                device(s, z, (x + dx) % NX, c),
            ).wait_recv()

    def z_ref(self, h, origin):
        _, _, x, c = place()
        return self.kv[0].at[c, origin, x] if h == 0 else self.kv[1].at[c, origin]

    def along_z(self, h, d, way):
        zsend, zrecv = self.sems[:2]
        s, z, x, c = place()
        origin = (z - way * d + self.planes) % self.planes
        self.go(
            self.z_ref(h, origin), zsend.at[h, (way + 1) // 2, d], zrecv.at[h, origin],
            device(s, (z + way + self.planes) % self.planes, x, c),
        )

    def await_z(self, h, d, way):
        zsend, zrecv = self.sems[:2]
        s, z, x, c = place()
        origin = (z - way * d + self.planes) % self.planes
        ref = self.z_ref(h, origin)
        remote(
            ref, ref, zsend.at[h, (way + 1) // 2, d], zrecv.at[h, origin], device(s, origin, x, c)
        ).wait_recv()
        return origin

    def swap(self, h, origin):
        _, _, _, _, csend, crecv = self.sems
        s, z, x, c = place()
        self.go(
            self.kv[h].at[c, origin], csend.at[h, origin], crecv.at[h, origin],
            device(s, z, x, 1 - c),
        )

    def reach(self, way):
        return self.planes // 2 if way == 1 else (self.planes - 1) // 2

    def start(self):
        _, z, x, c = place()
        self.along_x(1, z, 0)
        for way in (1, -1):
            if self.reach(way) > 0:
                self.along_z(0, 0, way)
        self.along_x(0, z, 0)

    def turn(self):
        z = place()[1]
        self.await_x(1, z, 0)
        for way in (1, -1):
            if self.reach(way) > 0:
                self.along_z(1, 0, way)
        self.swap(1, z)

    def step(self, d):
        for h in (0, 1):
            for way in (1, -1):
                if d <= self.reach(way):
                    origin = self.await_z(h, d, way)
                    if d < self.reach(way):
                        self.along_z(h, d, way)
                    if h == 0:
                        self.along_x(0, origin, d if way == 1 else self.planes - d)
                    else:
                        self.swap(1, origin)

    def settle(self):
        z = place()[1]
        for d in range(self.planes // 2 + 1):
            for way in (1, -1):
                if d <= self.reach(way) and (d > 0 or way == 1):
                    origin = (z - way * d + self.planes) % self.planes
                    self.await_x(0, origin, d if way == 1 else self.planes - d)
                    self.swap(0, origin)

    def ready(self, h):
        _, _, _, _, csend, crecv = self.sems
        s, z, x, c = place()
        for k in range(self.planes):
            ref = self.kv[h].at[1 - c, k]
            remote(ref, ref, csend.at[h, k], crecv.at[h, k], device(s, z, x, 1 - c)).wait_recv()

    def drain(self):
        for copy in self.started:
            copy.wait_send()

    @staticmethod
    def scratch(planes):
        return [
            dma(2, 2, planes), dma(2, planes), dma(2, planes, NX - 1), dma(2, planes, NX),
            dma(2, planes), dma(2, planes),
        ]


def join(first, second, half):
    upper = iota(first.shape, 0) < 4
    if half == 0:
        return jnp.where(upper, first, pltpu.roll(second, 4, 0))
    return jnp.where(upper, pltpu.roll(first, 4, 0), second)


class Dispatch:
    def __init__(
        self, send_ref, zbuf, shared, main, tail, zsend, zrecv, xsend, xrecv, tsend, trecv, local
    ):
        self.refs = (send_ref, zbuf, shared, main, tail)
        self.sems = (zsend, zrecv, xsend, xrecv, tsend, trecv, local)
        self.planes = send_ref.shape[0]
        self.started = []
        self.local = []

    def send(self, d):
        send_ref, zbuf = self.refs[:2]
        zsend, zrecv = self.sems[:2]
        s, z, x, c = place()
        to = (z + d) % self.planes
        copy = remote(
            send_ref.at[to], zbuf.at[z], zsend.at[d], zrecv.at[z], device(s, to, x, c)
        )
        copy.start()
        self.started.append(copy)

    def send_stages(self, stages):
        for stage in stages:
            for d in stage:
                self.send(d)

    def forward_all(self, k):
        stages = stages_of(self.planes)
        for d in stages[k]:
            self.forward(d)
        for j in {0: (0,), 2: (1, 3), 3: (2,)}.get(k, ()):
            self.forward_tail(j)

    def forward(self, d):
        send_ref, zbuf, _, main, _ = self.refs
        zsend, zrecv, xsend, xrecv, _, _, local = self.sems
        s, z, x, c = place()
        origin = (z + d) % self.planes
        source = zbuf.at[origin]
        if d == 0:
            source = send_ref.at[z]
            zbuf[z, 4] = send_ref[z, 4]
        else:
            remote(
                send_ref.at[origin], zbuf.at[origin], zsend.at[d], zrecv.at[origin],
                device(s, origin, x, c),
            ).wait_recv()
        for dx in (2, 1, 3):
            to = (x + dx) % NX
            copy = remote(
                source.at[pl.ds(5 * (to // 2), 4)], main.at[x * self.planes + origin],
                xsend.at[dx - 1, d], xrecv.at[x, origin], device(s, z, to, c),
            )
            copy.start()
            self.started.append(copy)
        mine = pltpu.make_async_copy(
            source.at[pl.ds(5 * (x // 2), 4)], main.at[x * self.planes + origin], local.at[d]
        )
        mine.start()
        self.local.append(mine)

    def pair(self, j):
        half = self.planes // 2
        return (place()[1] // 2 + j) % half

    def forward_tail(self, j):
        _, zbuf, shared, _, tail = self.refs
        _, _, _, _, tsend, trecv, _ = self.sems
        s, z, x, c = place()
        half = self.planes // 2
        p = self.pair(j)
        first, second = zbuf[2 * p, 4].astype(F32), zbuf[2 * p + 1, 4].astype(F32)
        for h in range(2):
            shared[p, h] = join(first, second, h).astype(BF)
        for dx in (2, 1, 3):
            to = (x + dx) % NX
            copy = remote(
                shared.at[p, to // 2], tail.at[x * half + p], tsend.at[dx - 1, j],
                trecv.at[x, p], device(s, z, to, c),
            )
            copy.start()
            self.started.append(copy)
        tail[x * half + p] = shared[p, x // 2]

    def arrive(self):
        send_ref, zbuf, shared, main, tail = self.refs
        zsend, zrecv, xsend, xrecv, tsend, trecv, local = self.sems
        s, z, x, c = place()
        half = self.planes // 2
        for d in range(self.planes):
            origin = (z + d) % self.planes
            for dx in range(1, NX):
                source = (x + dx) % NX
                remote(
                    zbuf.at[origin, pl.ds(0, 4)], main.at[source * self.planes + origin],
                    xsend.at[dx - 1, d], xrecv.at[source, origin], device(s, z, source, c),
                ).wait_recv()
        for j in range(half):
            p = self.pair(j)
            for dx in range(1, NX):
                source = (x + dx) % NX
                remote(
                    shared.at[p, 0], tail.at[source * half + p], tsend.at[dx - 1, j],
                    trecv.at[source, p], device(s, z, source, c),
                ).wait_recv()
        for copy in self.local:
            copy.wait()

    def drain(self):
        for copy in self.started:
            copy.wait_send()

    @staticmethod
    def scratch(planes):
        half = planes // 2
        return [
            dma(planes), dma(planes), dma(NX - 1, planes), dma(NX, planes),
            dma(NX - 1, half), dma(NX, half), dma(planes),
        ]


class Return:
    def __init__(
        self, main, tail, pmain, ptail, stage, out_ref, by, xsend, xrecv, tsend, trecv, zsend, zrecv
    ):
        self.refs = (main, tail, pmain, ptail, stage, out_ref)
        self.sems = (xsend, xrecv, tsend, trecv, zsend, zrecv)
        self.planes = stage.shape[0]
        self.by = by
        self.started = []

    def order(self):
        half = self.planes // 2
        return sorted(range(half), key=lambda j: -min(j, half - j))

    def pair(self, j):
        half = self.planes // 2
        return (place()[1] // 2 + j) % half

    def messages(self, j, mine):
        main, tail, pmain, ptail, _, _ = self.refs
        xsend, xrecv, tsend, trecv, _, _ = self.sems
        half = self.planes // 2
        p = self.pair(j)
        for dx in (2, 1, 3):
            other = (place()[2] + dx) % NX
            left = other if mine else place()[2]
            spot = place()[2] if mine else other
            for k in range(2):
                origin = 2 * p + k
                yield (
                    main.at[left * self.planes + origin], pmain.at[spot * self.planes + origin],
                    xsend.at[dx - 1, 2 * j + k], xrecv.at[spot, origin], other,
                )
            yield (
                tail.at[left * half + p], ptail.at[spot * half + p],
                tsend.at[dx - 1, j], trecv.at[spot, p], other,
            )

    def send(self, j):
        s, z, x, c = place()
        for source, target, sent, came, other in self.messages(j, True):
            copy = remote(source, target, sent, came, device(s, z, other, c))
            copy.start()
            self.started.append(copy)

    def forward(self, j):
        main, tail, pmain, ptail, stage, out_ref = self.refs
        _, _, _, _, zsend, zrecv = self.sems
        s, z, x, c = place()
        half = self.planes // 2
        p = self.pair(j)
        for k in range(2):
            mine = x * self.planes + 2 * p + k
            pmain[mine] = main[mine]
        ptail[x * half + p] = tail[x * half + p]
        for source, target, sent, came, other in self.messages(j, False):
            remote(source, target, sent, came, device(s, z, other, c)).wait_recv()

        def last(source):
            return ptail[source * half + p].astype(F32)

        first, second = last(0) + last(1), last(2) + last(3)
        sections = lax.axis_size("section")
        for k in range(2):
            origin = 2 * p + k

            def piece(source, q):
                return pmain[source * self.planes + origin, q].astype(F32)

            for q in range(QUARTERS):
                stage[origin, q] = (piece(0, q) + piece(1, q)).astype(BF)
                stage[origin, 5 + q] = (piece(2, q) + piece(3, q)).astype(BF)
            stage[origin, 4] = join(first, second, k).astype(BF)
            copy = remote(
                stage.at[origin], out_ref.at[z], zsend.at[2 * j + k], zrecv.at[z],
                device((s + self.by + sections) % sections, origin, x, c),
            )
            copy.start()
            self.started.append(copy)

    def arrive(self):
        stage, out_ref = self.refs[4:]
        zsend, zrecv = self.sems[4:]
        s, z, x, c = place()
        sections = lax.axis_size("section")
        for d in range(self.planes):
            origin = (z + d) % self.planes
            remote(
                stage.at[origin], out_ref.at[origin], zsend.at[d], zrecv.at[origin],
                device((s - self.by + sections) % sections, origin, x, c),
            ).wait_recv()

    def drain(self):
        for copy in self.started:
            copy.wait_send()

    @staticmethod
    def scratch(planes):
        half = planes // 2
        return [
            dma(NX - 1, planes), dma(NX, planes), dma(NX - 1, half), dma(NX, half),
            dma(planes), dma(planes),
        ]


def everyone(planes, sections):
    s, z, x, c = place()
    peers = [device(s, (z + d) % planes, x, c) for d in range(1, planes)]
    peers += [device(s, z, (x + d) % NX, c) for d in range(1, NX)]
    peers += [
        device((s + by) % sections, (z + d) % planes, x, c)
        for by in (1, sections - 1) for d in range(planes)
    ]
    return peers + [device(s, z, x, 1 - c)]


def hand_over(refs, outs, send, recv, target):
    copies = []
    for i, (ref, out) in enumerate(zip(refs, outs)):
        copy = remote(ref, out, send.at[i], recv.at[i], target)
        copy.start()
        copies.append(copy)
    return copies


NAMES = (
    "mid", "grad", "query", "entry", "own_g", "own_u", "own_d", "other_g", "other_u", "other_d",
    "kv0", "kv1", "total", "middle", "rows0", "rows1", "rows2", "zbuf0", "zbuf1", "zbuf2", "recv0",
    "recv1", "recv2", "part0", "part1", "pbuf0", "pbuf1", "stage0", "stage1", "back_in",
    "last0", "last1", "last2", "plast0", "plast1", "blast0", "blast1",
    "shared0", "shared1", "shared2",
    "mid_in", "grad_in", "gain_in", "b_meta", "f_meta", "b_meta_in", "result",
)


def main_kernel(
    sel, kv_in, gain, f_route, f_gate, b_route, b_gate,
    mid_hbm, grad_hbm, query_hbm, entry_hbm, wg, wu, wd,
    result_out, middle_out, f_meta_out, front_out,
    *scratch,
):
    v = dict(zip(NAMES, scratch))
    sems = list(scratch[len(NAMES) :])
    s, z, x, c = place()
    sections = lax.axis_size("section")
    planes = v["rows0"].shape[0]
    width = v["rows0"].shape[3]
    experts = planes * 2
    load, csend, crecv, ysend, yrecv = sems[:5]
    sems = sems[5:]
    kv = (v["kv0"], v["kv1"])
    gather = Gather(kv, *sems[:6])
    sends = [
        Dispatch(
            v[f"rows{i}"], v[f"zbuf{i}"], v[f"shared{i}"], v[f"recv{i}"], v[f"last{i}"],
            *sems[6 + 7 * i : 13 + 7 * i],
        )
        for i in range(3)
    ]
    ones, twos, front = sends
    back_ret, front_ret = [
        Return(
            v[f"part{i}"], v[f"plast{i}"], v[f"pbuf{i}"], v[f"blast{i}"], v[f"stage{i}"],
            (v["back_in"], front_out)[i], (-1, 1)[i], *sems[27 + 6 * i : 33 + 6 * i],
        )
        for i in range(2)
    ]

    local = []
    for i, (source, name) in enumerate(
        zip(
            (mid_hbm, grad_hbm, query_hbm, entry_hbm, wg, wu, wd),
            ("mid", "grad", "query", "entry", "own_g", "own_u", "own_d"),
        )
    ):
        copy = pltpu.make_async_copy(source, v[name], load.at[i])
        copy.start()
        local.append(copy)
    for head in range(KV_HEADS):
        for w in range(2):
            kv[head][c, z, x, w] = kv_in[w * KV_HEADS + head]
    for name, gate_ref, route_ref in (("b_meta", b_gate, b_route), ("f_meta", f_gate, f_route)):
        v[name][...] = jnp.zeros_like(v[name])
        v[name][0:1] = gate_ref[...]
        v[name][1:2] = route_ref[...].astype(F32)
    v["total"][...] = jnp.zeros_like(v["total"])
    greet(everyone(planes, sections))
    stages = stages_of(planes)
    gather.start()
    local[0].wait()
    pack(b_route[...], experts, normed_rows(v["mid"], gain, width), v["rows0"])
    ones.send_stages(stages[:2])
    ones.forward(0)
    gather.turn()
    gate = as_column(b_gate[...])
    local[1].wait()

    def scaled(q):
        return (gate * v["grad"][:, quarter(q, width)].astype(F32)).astype(BF)

    pack(b_route[...], experts, scaled, v["rows1"])
    twos.forward(0)
    before = device((s + sections - 1) % sections, z, x, c)
    after = device((s + 1) % sections, z, x, c)
    shipped = hand_over(
        (v["mid"], v["grad"], gain, v["b_meta"]),
        (v["mid_in"], v["grad_in"], v["gain_in"], v["b_meta_in"]),
        ysend.at[0], yrecv.at[0], before,
    )
    gather.step(1)
    ones.forward_all(0)
    ones.send_stages(stages[2:3])
    ones.forward_all(1)
    gather.step(2)
    ones.send_stages(stages[3:4])
    twos.send_stages(stages[0:1])
    ones.forward_all(2)
    gather.step(3)
    twos.send_stages(stages[1:3])
    ones.forward_all(3)
    twos.forward_all(0)
    gather.step(4)
    twos.send_stages(stages[3:4])
    twos.forward_all(1)
    gather.settle()
    weights = hand_over(
        (wg, wu, wd), (v["other_g"], v["other_u"], v["other_d"]), csend, crecv,
        device(s, z, x, 1 - c),
    )
    for copy in local[2:4]:
        copy.wait()
    blocks = v["query"].shape[0] // BLK
    first = lax.axis_index("expert") * blocks
    for head in (1, 0):
        gather.ready(head)
        for b in range(blocks):
            attend(b * KV_HEADS + head, first, sel, v["query"], kv, v["total"])
        if head == 1:
            twos.forward_all(2)
    for q in range(QUARTERS):
        cols = quarter(q, width)
        v["middle"][:, cols] = (
            v["entry"][:, cols].astype(F32) + v["total"][:, cols]
        ).astype(BF)
    pack(f_route[...], experts, normed_rows(v["middle"], gain, width), v["rows2"])
    front.send_stages(stages)
    front.forward(0)
    twos.forward_all(3)
    shipped += hand_over(
        (v["middle"], v["f_meta"]), (middle_out, f_meta_out), ysend.at[1], yrecv.at[1], after
    )
    front.forward_all(0)
    ones.arrive()
    twos.arrive()
    for copy in local[4:]:
        copy.wait()
    for copy in weights:
        copy.wait()
    own = (v["own_g"], v["own_u"], v["own_d"])
    other = (v["other_g"], v["other_u"], v["other_d"])
    backward_experts(
        (v["recv0"], v["last0"]), (v["recv1"], v["last1"]), own, other, (v["part0"], v["plast0"])
    )
    turns = back_ret.order()
    flow = Flow([(back_ret, d) for d in turns], 2)
    flow.open()
    front.forward_all(1)
    front.forward_all(2)
    flow.turn()
    front.forward_all(3)
    flow.turn()
    front.arrive()
    forward_experts((v["recv2"], v["last2"]), own, other, (v["part1"], v["plast1"]))
    flow.more([(front_ret, d) for d in turns])
    flow.turn(flow.left() - len(turns) // 2)
    back_ret.arrive()
    for copy in shipped:
        copy.wait()
    back_last(
        v["mid_in"], v["grad_in"], v["gain_in"], v["back_in"], v["b_meta_in"],
        v["result"], v["total"],
    )
    last = pltpu.make_async_copy(v["result"], result_out, load.at[7])
    last.start()
    flow.turn(flow.left())
    front_ret.arrive()
    last.wait()
    for one in (gather, ones, twos, front, back_ret, front_ret):
        one.drain()


ANY = pl.BlockSpec(memory_space=pl.ANY)
VMEM = pl.BlockSpec(memory_space=pltpu.VMEM)
SMEM = pl.BlockSpec(memory_space=pltpu.SMEM)


def shards(
    front_input, queries, keys_values, selected_blocks, front_route, front_gate,
    back_middle, back_grad, back_route, back_gate, norm_gain, gate_slice, up_slice, down_slice,
):
    tokens, features = front_input.shape[1:]
    planes = lax.axis_size("expert") // (2 * NX)
    width = features // QUARTERS
    kv = keys_values[0].T.reshape(2 * KV_HEADS, HEAD_DIM, tokens)
    message = pltpu.VMEM((planes, 9, 8, width), BF)
    arrived = pltpu.VMEM((NX * planes, QUARTERS, 8, width), BF)
    lasts = pltpu.VMEM((NX * planes // 2, 8, width), BF)
    rows = pltpu.VMEM((tokens, features), BF)
    tall = pltpu.VMEM(gate_slice.shape[2:], BF)
    flat = pltpu.VMEM(down_slice.shape[2:], BF)
    meta = pltpu.VMEM((8, tokens), F32)
    half_kv = pltpu.VMEM((2, planes, NX, 2, HEAD_DIM, tokens), BF)
    shapes = dict(
        mid=rows, grad=rows, query=rows, entry=rows, own_g=tall, own_u=tall, own_d=flat,
        other_g=tall, other_u=tall, other_d=flat,
        kv0=half_kv, kv1=half_kv,
        total=pltpu.VMEM((tokens, features), F32), middle=rows,
        back_in=message, mid_in=rows, grad_in=rows, gain_in=pltpu.VMEM((1, features), F32),
        b_meta=meta, f_meta=meta, b_meta_in=meta, result=rows,
    )
    for i in range(3):
        shapes[f"rows{i}"] = shapes[f"zbuf{i}"] = message
        shapes[f"recv{i}"] = shapes[f"part{i}"] = shapes[f"pbuf{i}"] = arrived
        shapes[f"stage{i}"] = message
        shapes[f"last{i}"] = shapes[f"plast{i}"] = shapes[f"blast{i}"] = lasts
        shapes[f"shared{i}"] = pltpu.VMEM((planes // 2, 2, 8, width), BF)
    result, middle, f_meta, front = pl.pallas_call(
        main_kernel,
        out_shape=[
            jax.ShapeDtypeStruct((tokens, features), BF),
            jax.ShapeDtypeStruct((tokens, features), BF),
            jax.ShapeDtypeStruct((8, tokens), F32),
            jax.ShapeDtypeStruct((planes, 9, 8, width), BF),
        ],
        in_specs=[SMEM] + [VMEM] * 6 + [ANY] * 7,
        out_specs=[ANY] * 4,
        scratch_shapes=[shapes[name] for name in NAMES]
        + [dma(8), dma(3), dma(3), dma(2, 4), dma(2, 4)]
        + Gather.scratch(planes) + Dispatch.scratch(planes) * 3 + Return.scratch(planes) * 2,
        compiler_params=pltpu.CompilerParams(
            collective_id=0, has_side_effects=True, vmem_limit_bytes=63 << 20
        ),
        name="layer",
    )(
        selected_blocks[0], kv, norm_gain,
        front_route.reshape(1, tokens), front_gate.reshape(1, tokens),
        back_route.reshape(1, tokens), back_gate.reshape(1, tokens),
        back_middle[0], back_grad[0], queries[0], front_input[0],
        gate_slice[0, 0], up_slice[0, 0], down_slice[0, 0],
    )
    front_output, back_output = pl.pallas_call(
        front_last_kernel,
        out_shape=[jax.ShapeDtypeStruct((tokens, features), BF)] * 2,
        in_specs=[ANY] * 4,
        out_specs=[ANY] * 2,
        scratch_shapes=[rows, message, meta, rows, rows, dma(5 + QUARTERS)],
        compiler_params=pltpu.CompilerParams(vmem_limit_bytes=63 << 20),
        name="front_last",
    )(middle, front, f_meta, result)
    return (front_output[None], back_output[None])


def solution(mesh):
    rows = P("section", "expert", None)
    wide = P("section", "expert", None, None)
    return jax.shard_map(
        shards,
        mesh=mesh,
        in_specs=(rows, rows, rows, wide, rows, rows, rows, rows, rows, rows,
                  P("section", None), wide, wide, wide),
        out_specs=(rows, rows),
        check_vma=False,
    )
```

time: 279 us -> 194 us (0.70)
  Pallas kernels: 234 us -> 192 us
  local copies, waits for them, and re-layouts: 25.8 us -> 0 us
  between operations: 14.2 us -> 0.8 us
    pallas_call x9 -> x2, Pallas kernels: 234 us -> 192 us  [the longest x1 188 us: shards(): pl.pallas_call(main_kernel, out_shape=[jax.ShapeDtypeStruct((tokens, feat...]
    unnamed x63 -> x0, local copies, waits for them, and re-layouts: 24.2 us -> none
  transfers between devices with their start and end apart: 1 -> 0, of which waited for: 0 -> 0; matrix products, arithmetic and copies ran while one was open for 1% -> 0% of each run, Pallas kernels for 41% -> 0%
where the time goes in v2:
time: 194 us; the launch traced here: 193 us
  Pallas kernels  192 us (99%)
    pallas_call x1, Pallas kernels, shards(): pl.pallas_call(main_kernel, out_shape=[jax.ShapeDtypeStruct((tokens, feat...  188 us

profile of v2, /device:TPU:34, one launch (start us, length us, event | category | flops | bytes accessed | tf_op | source)
XLA Modules:
  0.0 192.5 jit_solution(3368006106327120857)
XLA Ops:
  0.6 188.3 %layer.1 = (bf16[128,3584]{1,0:T(8,128)(2,1)}, bf16[128,3584]{1,0:T(8,128)(2,1)}, f32[8,128]{1,0:T(8,128)}, bf16[8,9,8,896]{3,2,1,0:T(8,128)(2,1)}) custom-call(s32[2,2,4]{2,1,0:T(2,128)} %bitcast.27, bf16[4,112,128]{2,1,0:T(8,128)(2,1)} %bitcast.26, f32[1,3584]{1,0:T(1,128)} %gain.1, s32[1,128]{1,0:T(1,128)} %bitcast.28, f32[1,128]{1,0:T(1,128)} %bitcast.29, ...), custom_call_target="tpu_custom_call" | custom-call | tf_op jit(solution)/shard_map/layer/pallas_call | solution.py:933
  189.0 3.4 %front_last.1 = (bf16[128,3584]{1,0:T(8,128)(2,1)}, bf16[128,3584]{1,0:T(8,128)(2,1)}) custom-call(bf16[128,3584]{1,0:T(8,128)(2,1)} %get-tuple-element.8.middle_hbm, bf16[8,9,8,896]{3,2,1,0:T(8,128)(2,1)} %get-tuple-element.9.back_hbm, f32[8,128]{1,0:T(8,128)} %get-tuple-element.10.meta_hbm, bf16[128,3584]{1,0:T(8,128)(2,1)} %get-tuple-element.11.done_hbm), custom_call_target="tpu_custom_call" | custom-call | tf_op jit(solution)/shard_map/front_last/pallas_call | solution.py:957

commit v3 on v2

--- a/solution.py
+++ b/solution.py
@@ -160,12 +160,18 @@
     return jnp.where(col == row * 4 + q, 1.0, 0.0).astype(BF)
 
 
-def rows_for_expert(main_ref, tail_ref, q):
+def gather_rows(recv, rows_ref):
+    main_ref, tail_ref = recv
     count, width = main_ref.shape[0], main_ref.shape[3]
-    main = main_ref[:, q].astype(F32).reshape(count * 8, width).astype(BF)
     last = tail_ref[...].astype(F32).reshape(count * 4, width).astype(BF)
-    tail = jnp.dot(tail_select(count, q), last, preferred_element_type=F32).astype(BF)
-    return jnp.concatenate([main, tail], axis=0)
+    for q in range(QUARTERS):
+        cols = quarter(q, width)
+        rows_ref[: count * 8, cols] = (
+            main_ref[:, q].astype(F32).reshape(count * 8, width).astype(BF)
+        )
+        rows_ref[count * 8 :, cols] = jnp.dot(
+            tail_select(count, q), last, preferred_element_type=F32
+        ).astype(BF)
 
 
 def store_for_source(main_ref, q, value, tail_total):
@@ -178,59 +184,42 @@
     return spread if tail_total is None else tail_total + spread
 
 
-def forward_experts(recv, own, other, out):
+def forward_experts(recv, rows_ref, wide_ref, down_ref, out):
+    gather_rows(recv, rows_ref)
     width = recv[0].shape[3]
-    sides = (own, other)
-    gates, ups = [None, None], [None, None]
-    for q in range(QUARTERS):
-        rows = rows_for_expert(*recv, q)
-        part = quarter(q, width)
-        for i, (g, u, _) in enumerate(sides):
-            gate = jnp.dot(rows, g[part], preferred_element_type=F32)
-            up = jnp.dot(rows, u[part], preferred_element_type=F32)
-            gates[i] = gate if gates[i] is None else gates[i] + gate
-            ups[i] = up if ups[i] is None else ups[i] + up
-    hidden = [(v / (1.0 + jnp.exp(-v)) * u).astype(BF) for v, u in zip(gates, ups)]
+    half = wide_ref.shape[1] // 2
+    both = jnp.dot(rows_ref[...], wide_ref[...], preferred_element_type=F32)
+    gate, up = both[:, :half], both[:, half:]
+    hidden = (gate / (1.0 + jnp.exp(-gate)) * up).astype(BF)
     tail = None
     for q in range(QUARTERS):
-        part = quarter(q, width)
-        value = jnp.dot(hidden[0], own[2][:, part], preferred_element_type=F32) + jnp.dot(
-            hidden[1], other[2][:, part], preferred_element_type=F32
-        )
+        value = jnp.dot(hidden, down_ref[:, quarter(q, width)], preferred_element_type=F32)
         tail = store_for_source(out[0], q, value, tail)
     out[1][...] = tail.reshape(out[1].shape).astype(BF)
 
 
-def backward_experts(recv, recv_grad, own, other, out):
+def backward_experts(recv, recv_grad, rows_ref, grads_ref, wide_ref, down_ref, out):
+    gather_rows(recv, rows_ref)
+    gather_rows(recv_grad, grads_ref)
     width = recv[0].shape[3]
+    half = wide_ref.shape[1] // 2
     last = (((1,), (1,)), ((), ()))
-    sides = (own, other)
-    gates, ups, downs = [None, None], [None, None], [None, None]
-    for q in range(QUARTERS):
-        rows = rows_for_expert(*recv, q)
-        grads = rows_for_expert(*recv_grad, q)
-        part = quarter(q, width)
-        for i, (g, u, d) in enumerate(sides):
-            gate = jnp.dot(rows, g[part], preferred_element_type=F32)
-            up = jnp.dot(rows, u[part], preferred_element_type=F32)
-            down = lax.dot_general(grads, d[:, part], last, preferred_element_type=F32)
-            gates[i] = gate if gates[i] is None else gates[i] + gate
-            ups[i] = up if ups[i] is None else ups[i] + up
-            downs[i] = down if downs[i] is None else downs[i] + down
-    gate_grads, up_grads = [], []
-    for gate, up, down in zip(gates, ups, downs):
-        sigmoid = 1.0 / (1.0 + jnp.exp(-gate))
-        gate_grads.append((down * up * (sigmoid * (1.0 + gate * (1.0 - sigmoid)))).astype(BF))
-        up_grads.append((down * (gate * sigmoid)).astype(BF))
+    both = jnp.dot(rows_ref[...], wide_ref[...], preferred_element_type=F32)
+    gate, up = both[:, :half], both[:, half:]
+    down = lax.dot_general(grads_ref[...], down_ref[...], last, preferred_element_type=F32)
+    sigmoid = 1.0 / (1.0 + jnp.exp(-gate))
+    grads = jnp.concatenate(
+        [
+            (down * up * (sigmoid * (1.0 + gate * (1.0 - sigmoid)))).astype(BF),
+            (down * (gate * sigmoid)).astype(BF),
+        ],
+        axis=1,
+    )
     tail = None
     for q in range(QUARTERS):
-        part = quarter(q, width)
-        value = None
-        for i, (g, u, _) in enumerate(sides):
-            more = lax.dot_general(
-                gate_grads[i], g[part], last, preferred_element_type=F32
-            ) + lax.dot_general(up_grads[i], u[part], last, preferred_element_type=F32)
-            value = more if value is None else value + more
+        value = lax.dot_general(
+            grads, wide_ref[quarter(q, width)], last, preferred_element_type=F32
+        )
         tail = store_for_source(out[0], q, value, tail)
     out[1][...] = tail.reshape(out[1].shape).astype(BF)
 
@@ -730,7 +719,7 @@
 
 
 NAMES = (
-    "mid", "grad", "query", "entry", "own_g", "own_u", "own_d", "other_g", "other_u", "other_d",
+    "mid", "grad", "query", "entry", "wide", "down", "expert0", "expert1",
     "kv0", "kv1", "total", "middle", "rows0", "rows1", "rows2", "zbuf0", "zbuf1", "zbuf2", "recv0",
     "recv1", "recv2", "part0", "part1", "pbuf0", "pbuf1", "stage0", "stage1", "back_in",
     "last0", "last1", "last2", "plast0", "plast1", "blast0", "blast1",
@@ -773,13 +762,14 @@
     ]
 
     local = []
-    for i, (source, name) in enumerate(
-        zip(
-            (mid_hbm, grad_hbm, query_hbm, entry_hbm, wg, wu, wd),
-            ("mid", "grad", "query", "entry", "own_g", "own_u", "own_d"),
-        )
+    hidden = wg.shape[1]
+    places = [v["wide"].at[:, pl.ds(k * hidden, hidden)] for k in range(4)]
+    places += [v["down"].at[pl.ds(k * hidden, hidden)] for k in range(2)]
+    targets = [v[name] for name in ("mid", "grad", "query", "entry")] + places[::2]
+    for i, (source, target) in enumerate(
+        zip((mid_hbm, grad_hbm, query_hbm, entry_hbm, wg, wu, wd), targets)
     ):
-        copy = pltpu.make_async_copy(source, v[name], load.at[i])
+        copy = pltpu.make_async_copy(source, target, load.at[i])
         copy.start()
         local.append(copy)
     for head in range(KV_HEADS):
@@ -793,11 +783,11 @@
     greet(everyone(planes, sections))
     stages = stages_of(planes)
     gather.start()
+    gather.turn()
     local[0].wait()
     pack(b_route[...], experts, normed_rows(v["mid"], gain, width), v["rows0"])
-    ones.send_stages(stages[:2])
+    ones.send_stages(stages[:1])
     ones.forward(0)
-    gather.turn()
     gate = as_column(b_gate[...])
     local[1].wait()
 
@@ -805,34 +795,33 @@
         return (gate * v["grad"][:, quarter(q, width)].astype(F32)).astype(BF)
 
     pack(b_route[...], experts, scaled, v["rows1"])
-    twos.forward(0)
     before = device((s + sections - 1) % sections, z, x, c)
     after = device((s + 1) % sections, z, x, c)
+    gather.step(1)
+    ones.send_stages(stages[1:2])
+    ones.forward_all(0)
+    gather.step(2)
+    ones.send_stages(stages[2:3])
+    twos.forward(0)
+    ones.forward_all(1)
+    gather.step(3)
+    ones.send_stages(stages[3:4])
+    gather.step(4)
+    twos.send_stages(stages)
+    ones.forward_all(2)
+    gather.settle()
     shipped = hand_over(
         (v["mid"], v["grad"], gain, v["b_meta"]),
         (v["mid_in"], v["grad_in"], v["gain_in"], v["b_meta_in"]),
         ysend.at[0], yrecv.at[0], before,
     )
-    gather.step(1)
-    ones.forward_all(0)
-    ones.send_stages(stages[2:3])
-    ones.forward_all(1)
-    gather.step(2)
-    ones.send_stages(stages[3:4])
-    twos.send_stages(stages[0:1])
-    ones.forward_all(2)
-    gather.step(3)
-    twos.send_stages(stages[1:3])
+    weights = hand_over(
+        (wg, wu, wd), places[1::2], csend, crecv,
+        device(s, z, x, 1 - c),
+    )
     ones.forward_all(3)
     twos.forward_all(0)
-    gather.step(4)
-    twos.send_stages(stages[3:4])
     twos.forward_all(1)
-    gather.settle()
-    weights = hand_over(
-        (wg, wu, wd), (v["other_g"], v["other_u"], v["other_d"]), csend, crecv,
-        device(s, z, x, 1 - c),
-    )
     for copy in local[2:4]:
         copy.wait()
     blocks = v["query"].shape[0] // BLK
@@ -862,10 +851,9 @@
         copy.wait()
     for copy in weights:
         copy.wait()
-    own = (v["own_g"], v["own_u"], v["own_d"])
-    other = (v["other_g"], v["other_u"], v["other_d"])
     backward_experts(
-        (v["recv0"], v["last0"]), (v["recv1"], v["last1"]), own, other, (v["part0"], v["plast0"])
+        (v["recv0"], v["last0"]), (v["recv1"], v["last1"]), v["expert0"], v["expert1"],
+        v["wide"], v["down"], (v["part0"], v["plast0"]),
     )
     turns = back_ret.order()
     flow = Flow([(back_ret, d) for d in turns], 2)
@@ -876,7 +864,9 @@
     front.forward_all(3)
     flow.turn()
     front.arrive()
-    forward_experts((v["recv2"], v["last2"]), own, other, (v["part1"], v["plast1"]))
+    forward_experts(
+        (v["recv2"], v["last2"]), v["expert0"], v["wide"], v["down"], (v["part1"], v["plast1"])
+    )
     flow.more([(front_ret, d) for d in turns])
     flow.turn(flow.left() - len(turns) // 2)
     back_ret.arrive()
@@ -912,14 +902,14 @@
     arrived = pltpu.VMEM((NX * planes, QUARTERS, 8, width), BF)
     lasts = pltpu.VMEM((NX * planes // 2, 8, width), BF)
     rows = pltpu.VMEM((tokens, features), BF)
-    tall = pltpu.VMEM(gate_slice.shape[2:], BF)
-    flat = pltpu.VMEM(down_slice.shape[2:], BF)
+    many = pltpu.VMEM((NX * planes * 9, features), BF)
     meta = pltpu.VMEM((8, tokens), F32)
     half_kv = pltpu.VMEM((2, planes, NX, 2, HEAD_DIM, tokens), BF)
     shapes = dict(
-        mid=rows, grad=rows, query=rows, entry=rows, own_g=tall, own_u=tall, own_d=flat,
-        other_g=tall, other_u=tall, other_d=flat,
-        kv0=half_kv, kv1=half_kv,
+        mid=rows, grad=rows, query=rows, entry=rows,
+        wide=pltpu.VMEM((features, 4 * gate_slice.shape[3]), BF),
+        down=pltpu.VMEM((2 * gate_slice.shape[3], features), BF),
+        expert0=many, expert1=many, kv0=half_kv, kv1=half_kv,
         total=pltpu.VMEM((tokens, features), F32), middle=rows,
         back_in=message, mid_in=rows, grad_in=rows, gain_in=pltpu.VMEM((1, features), F32),
         b_meta=meta, f_meta=meta, b_meta_in=meta, result=rows,

time: 194 us -> 181 us (0.933)
  Pallas kernels: 192 us -> 179 us
    pallas_call x1, Pallas kernels: 188 us -> 175 us  [shards(): pl.pallas_call(main_kernel, out_shape=[jax.ShapeDtypeStruct((tokens, feat...]
where the time goes in v3:
time: 181 us; the launch traced here: 179 us
  Pallas kernels  179 us (99%)
    pallas_call x1, Pallas kernels, shards(): pl.pallas_call(main_kernel, out_shape=[jax.ShapeDtypeStruct((tokens, feat...  175 us

profile of v3, /device:TPU:34, one launch (start us, length us, event | category | flops | bytes accessed | tf_op | source)
XLA Modules:
  0.0 179.4 jit_solution(6126473210726966892)
XLA Ops:
  0.6 175.2 %layer.1 = (bf16[128,3584]{1,0:T(8,128)(2,1)}, bf16[128,3584]{1,0:T(8,128)(2,1)}, f32[8,128]{1,0:T(8,128)}, bf16[8,9,8,896]{3,2,1,0:T(8,128)(2,1)}) custom-call(s32[2,2,4]{2,1,0:T(2,128)} %bitcast.27, bf16[4,112,128]{2,1,0:T(8,128)(2,1)} %bitcast.26, f32[1,3584]{1,0:T(1,128)} %gain.1, s32[1,128]{1,0:T(1,128)} %bitcast.28, f32[1,128]{1,0:T(1,128)} %bitcast.29, ...), custom_call_target="tpu_custom_call" | custom-call | tf_op jit(solution)/shard_map/layer/pallas_call | solution.py:923
  175.9 3.4 %front_last.1 = (bf16[128,3584]{1,0:T(8,128)(2,1)}, bf16[128,3584]{1,0:T(8,128)(2,1)}) custom-call(bf16[128,3584]{1,0:T(8,128)(2,1)} %get-tuple-element.8.middle_hbm, bf16[8,9,8,896]{3,2,1,0:T(8,128)(2,1)} %get-tuple-element.9.back_hbm, f32[8,128]{1,0:T(8,128)} %get-tuple-element.10.meta_hbm, bf16[128,3584]{1,0:T(8,128)(2,1)} %get-tuple-element.11.done_hbm), custom_call_target="tpu_custom_call" | custom-call | tf_op jit(solution)/shard_map/front_last/pallas_call | solution.py:947

commit v4 on v3

--- a/solution.py
+++ b/solution.py
@@ -148,7 +148,7 @@
         scores = jnp.dot(query, key_moved, preferred_element_type=F32) * HEAD_DIM ** (-0.5)
         scores = jnp.where(allowed, scores, NEG)
         exp_scores = jnp.exp(scores - jnp.max(scores, axis=-1, keepdims=True))
-        weights = exp_scores / jnp.sum(exp_scores, axis=-1, keepdims=True)
+        weights = exp_scores * (1.0 / jnp.sum(exp_scores, axis=-1, keepdims=True))
         mixed = lax.dot_general(
             weights.astype(BF), value_moved, (((1,), (1,)), ((), ())), preferred_element_type=F32
         )
@@ -798,17 +798,16 @@
     before = device((s + sections - 1) % sections, z, x, c)
     after = device((s + 1) % sections, z, x, c)
     gather.step(1)
-    ones.send_stages(stages[1:2])
     ones.forward_all(0)
     gather.step(2)
+    ones.send_stages(stages[1:2])
+    gather.step(3)
     ones.send_stages(stages[2:3])
+    gather.step(4)
+    ones.send_stages(stages[3:4])
+    twos.send_stages(stages)
     twos.forward(0)
     ones.forward_all(1)
-    gather.step(3)
-    ones.send_stages(stages[3:4])
-    gather.step(4)
-    twos.send_stages(stages)
-    ones.forward_all(2)
     gather.settle()
     shipped = hand_over(
         (v["mid"], v["grad"], gain, v["b_meta"]),
@@ -819,9 +818,9 @@
         (wg, wu, wd), places[1::2], csend, crecv,
         device(s, z, x, 1 - c),
     )
+    ones.forward_all(2)
     ones.forward_all(3)
     twos.forward_all(0)
-    twos.forward_all(1)
     for copy in local[2:4]:
         copy.wait()
     blocks = v["query"].shape[0] // BLK
@@ -831,7 +830,7 @@
         for b in range(blocks):
             attend(b * KV_HEADS + head, first, sel, v["query"], kv, v["total"])
         if head == 1:
-            twos.forward_all(2)
+            twos.forward_all(1)
     for q in range(QUARTERS):
         cols = quarter(q, width)
         v["middle"][:, cols] = (
@@ -840,11 +839,13 @@
     pack(f_route[...], experts, normed_rows(v["middle"], gain, width), v["rows2"])
     front.send_stages(stages)
     front.forward(0)
+    twos.forward_all(2)
     twos.forward_all(3)
     shipped += hand_over(
         (v["middle"], v["f_meta"]), (middle_out, f_meta_out), ysend.at[1], yrecv.at[1], after
     )
-    front.forward_all(0)
+    for k in range(len(stages)):
+        front.forward_all(k)
     ones.arrive()
     twos.arrive()
     for copy in local[4:]:
@@ -856,13 +857,8 @@
         v["wide"], v["down"], (v["part0"], v["plast0"]),
     )
     turns = back_ret.order()
-    flow = Flow([(back_ret, d) for d in turns], 2)
+    flow = Flow([(back_ret, d) for d in turns], 3)
     flow.open()
-    front.forward_all(1)
-    front.forward_all(2)
-    flow.turn()
-    front.forward_all(3)
-    flow.turn()
     front.arrive()
     forward_experts(
         (v["recv2"], v["last2"]), v["expert0"], v["wide"], v["down"], (v["part1"], v["plast1"])

time: 181 us -> 178 us (0.983)
  Pallas kernels: 179 us -> 177 us
    pallas_call x1, Pallas kernels: 175 us -> 173 us  [shards(): pl.pallas_call(main_kernel, out_shape=[jax.ShapeDtypeStruct((tokens, feat...]
where the time goes in v4:
time: 178 us; the launch traced here: 177 us
  Pallas kernels  177 us (99%)
    pallas_call x1, Pallas kernels, shards(): pl.pallas_call(main_kernel, out_shape=[jax.ShapeDtypeStruct((tokens, feat...  173 us

profile of v4, /device:TPU:34, one launch (start us, length us, event | category | flops | bytes accessed | tf_op | source)
XLA Modules:
  0.0 177.4 jit_solution(12954459482672990156)
XLA Ops:
  0.6 173.2 %layer.1 = (bf16[128,3584]{1,0:T(8,128)(2,1)}, bf16[128,3584]{1,0:T(8,128)(2,1)}, f32[8,128]{1,0:T(8,128)}, bf16[8,9,8,896]{3,2,1,0:T(8,128)(2,1)}) custom-call(s32[2,2,4]{2,1,0:T(2,128)} %bitcast.27, bf16[4,112,128]{2,1,0:T(8,128)(2,1)} %bitcast.26, f32[1,3584]{1,0:T(1,128)} %gain.1, s32[1,128]{1,0:T(1,128)} %bitcast.28, f32[1,128]{1,0:T(1,128)} %bitcast.29, ...), custom_call_target="tpu_custom_call" | custom-call | tf_op jit(solution)/shard_map/layer/pallas_call | solution.py:919
  173.9 3.4 %front_last.1 = (bf16[128,3584]{1,0:T(8,128)(2,1)}, bf16[128,3584]{1,0:T(8,128)(2,1)}) custom-call(bf16[128,3584]{1,0:T(8,128)(2,1)} %get-tuple-element.8.middle_hbm, bf16[8,9,8,896]{3,2,1,0:T(8,128)(2,1)} %get-tuple-element.9.back_hbm, f32[8,128]{1,0:T(8,128)} %get-tuple-element.10.meta_hbm, bf16[128,3584]{1,0:T(8,128)(2,1)} %get-tuple-element.11.done_hbm), custom_call_target="tpu_custom_call" | custom-call | tf_op jit(solution)/shard_map/front_last/pallas_call | solution.py:943
